TPU v7x, 256 devices: a whole 4x4x8 slice. The times are simulated.
256 devices in a mesh: slab: 32 (over x_hi, z, core), coil: 8 (over x_lo, y).
Axes of the slice: x: 4 (x_hi: 2, x_lo: 2; x = x_hi * 2 + x_lo), y: 4, z: 8, core: 2. Of those that a mesh axis runs over, the one named last changes fastest.
Arguments:
- current_image: bfloat16 [8, 5, 2, 2, 256, 384], P('coil', None, None, None, 'slab'), may hold values from -6 to 6
- coil_maps: bfloat16 [32, 2, 2, 256, 384], P(None, None, None, 'slab'), may hold values from -2.5 to 2.5
- measured: bfloat16 [8, 32, 5, 2, 2, 384, 256], P('coil', 'slab'), may hold values from -4 to 4
- sampling: int32 [8, 5, 384, 256], P('coil'), may hold values 0 or 1
- first_weight: bfloat16 [64, 10, 3, 3, 3], replicated, may hold values from -0.375 to 0.375
- first_bias: float32 [64], replicated, may hold values from -3 to 3
- second_weight: bfloat16 [10, 64, 3, 3, 3], replicated, may hold values from -0.15625 to 0.15625
- second_bias: float32 [10], replicated, may hold values from -3 to 3
Outputs:
- refined: bfloat16 [8, 5, 2, 2, 256, 384], P('coil', None, None, None, 'slab')
All inputs are finite; a program needn't handle non-finite values. No bound on the sum of `sampling` on one device may be relied on, other than what follows from the above.
Results may differ from a plain program's by a relative error of at most 0.014.
Values may be sent and summed in bfloat16 or wider, within the bound.
A program may use at most 128 MiB of HBM per device.

v0:
```python
import math

import jax
import jax.numpy as jnp
from jax import lax
from jax.sharding import PartitionSpec as P

NZ = 256


def with_halo(cells, sides, width):
    for axis, dim in sides:
        count = lax.axis_size(axis)
        ends = count - 1
        head = lax.slice_in_dim(cells, 0, width, axis=dim)
        tail = lax.slice_in_dim(cells, cells.shape[dim] - width, cells.shape[dim], axis=dim)
        cells = jnp.concatenate(
            [
                lax.ppermute(tail, axis, [(i, (i + 1) % count) for i in range(ends)]),
                cells,
                lax.ppermute(head, axis, [((i + 1) % count, i) for i in range(ends)]),
            ],
            axis=dim,
        )
    return cells


def dft_table(length, inverse):
    indices = jnp.arange(length, dtype=jnp.int32)
    wrapped = indices[:, None] * indices[None, :] % length
    angles = wrapped.astype(jnp.float32) * (2.0 * math.pi / length)
    factor = 1.0 / math.sqrt(length)
    cosine = jnp.cos(angles) * factor
    sine_part = jnp.sin(angles) * factor
    phase_sign = 1.0 if inverse else -1.0
    upper_rows = jnp.stack([cosine, phase_sign * sine_part], axis=1)
    lower_rows = jnp.stack([-phase_sign * sine_part, cosine], axis=1)
    return jnp.stack([upper_rows, lower_rows], axis=0).astype(jnp.bfloat16)


def coil_products(maps_part, image_part):
    maps_real = maps_part[:, 0][None, :, None].astype(jnp.float32)
    maps_imaginary = maps_part[:, 1][None, :, None].astype(jnp.float32)
    image_real = image_part[:, :, 0][:, None].astype(jnp.float32)
    image_imaginary = image_part[:, :, 1][:, None].astype(jnp.float32)
    real_part = maps_real * image_real - maps_imaginary * image_imaginary
    imaginary_part = maps_real * image_imaginary + maps_imaginary * image_real
    return jnp.stack([real_part, imaginary_part], axis=3).astype(jnp.bfloat16)


def transform(operand, matrix):
    return jnp.einsum("pcerxzy,ryqk->pceqxzk", operand, matrix, preferred_element_type=jnp.float32)


def combine_coils(maps_part, values):
    maps_real = maps_part[:, 0][None, :, None].astype(jnp.float32)
    maps_imaginary = maps_part[:, 1][None, :, None].astype(jnp.float32)
    real_sum = jnp.sum(maps_real * values[:, :, :, 0] + maps_imaginary * values[:, :, :, 1], axis=1)
    imaginary_sum = jnp.sum(
        maps_real * values[:, :, :, 1] - maps_imaginary * values[:, :, :, 0], axis=1
    )
    return jnp.stack([real_sum, imaginary_sum], axis=2)


def convolve(operand, weights):
    widened = jnp.pad(operand, ((0, 0), (0, 0), (0, 0), (0, 0), (1, 1)))
    return lax.conv_general_dilated(
        widened,
        weights,
        (1, 1, 1),
        "VALID",
        dimension_numbers=("DCNHW", "OIDHW", "DCNHW"),
        preferred_element_type=jnp.float32,
    )


def on_device(
    current_image,
    coil_maps,
    measured,
    sampling,
    first_weight,
    first_bias,
    second_weight,
    second_bias,
):
    forward_y = dft_table(current_image.shape[5], False)
    inverse_y = dft_table(current_image.shape[5], True)
    forward_z = dft_table(NZ, False)
    inverse_z = dft_table(NZ, True)
    sampled = sampling.astype(jnp.float32)[:, None, :, None, None]
    row_spectra = transform(coil_products(coil_maps, current_image), forward_y).astype(jnp.bfloat16)
    spectrum = jnp.einsum(
        "pcerxzk,rzqj->pceqxkj",
        lax.all_to_all(row_spectra, "slab", split_axis=1, concat_axis=5, tiled=True),
        forward_z,
        preferred_element_type=jnp.float32,
    )
    residual = (sampled * (spectrum - measured.astype(jnp.float32))).astype(jnp.bfloat16)
    depth_back = jnp.einsum(
        "pcerxkj,rjqz->pceqxzk", residual, inverse_z, preferred_element_type=jnp.float32
    ).astype(jnp.bfloat16)
    gradient = combine_coils(
        coil_maps,
        transform(
            lax.all_to_all(depth_back, "slab", split_axis=5, concat_axis=1, tiled=True), inverse_y
        ),
    )
    updated = (current_image.astype(jnp.float32) - gradient).astype(jnp.bfloat16)
    stacked = updated.reshape((updated.shape[0], 2 * updated.shape[1]) + updated.shape[3:])
    bias_first = first_bias[None, :, None, None, None]
    bordered = with_halo(stacked, (("slab", 3), ("coil", 0)), 1)
    hidden = jax.nn.relu(convolve(bordered, first_weight) + bias_first).astype(jnp.bfloat16)
    bordered_hidden = with_halo(hidden, (("slab", 3), ("coil", 0)), 1)
    second = convolve(bordered_hidden, second_weight)
    refined = stacked.astype(jnp.float32) + second + second_bias[None, :, None, None, None]
    return refined.astype(jnp.bfloat16).reshape(updated.shape)


def solution(mesh):
    in_specs = (
        P("coil", None, None, None, "slab", None),
        P(None, None, None, "slab", None),
        P("coil", "slab", None, None, None, None, None),
        P("coil", None, None, None),
        P(),
        P(),
        P(),
        P(),
    )
    out_specs = P("coil", None, None, None, "slab", None)
    return jax.shard_map(
        on_device, mesh=mesh, in_specs=in_specs, out_specs=out_specs, check_vma=False
    )
```

profile of v0, /device:TPU:35, one launch (start us, length us, event | category | flops | bytes accessed | tf_op | source)
XLA Modules:
  0.0 389.6 jit_solution(16283236424347183866)
XLA Ops:
  0.0 2.3 multiply_convert_fusion.2
  2.3 2.4 multiply_convert_fusion
  5.6 1.2 bitcast_convert_fusion.3
  7.4 1.1 fusion.41
  8.4 1.3 subtract_convert_fusion
  9.7 3.5 fusion.8
  13.2 3.3 copy.87
  16.5 11.0 %all-to-all-start = ((bf16[1,32,5,2,2,8,384]{6,5,4,2,3,0,1:T(8,128)(2,1)}), bf16[1,32,5,2,2,8,384]{6,5,4,2,3,0,1:T(8,128)(2,1)}, u32[]{:S(2)}, u32[]{:S(2)}) async-start(bf16[1,32,5,2,2,8,384]{6,5,4,2,3,0,1:T(8,128)(2,1)} %copy.87), calls=%async_computation | async-start | bytes 7864320 | tf_op jit(solution)/shard_map/all_to_all | solution.py:95
  27.5 1.7 convert_bitcast_fusion
  29.2 1.8 copy.82
  31.0 6.4 %copy.90 = bf16[1,1,5,2,2,384,256]{5,6,4,2,3,1,0:T(8,128)(2,1)} copy(bf16[1,1,5,2,2,384,256]{6,5,4,3,2,1,0:T(8,128)(2,1)} %param.10) | data formatting | bytes 7864320 | tf_op args[2]
  37.5 1.0 multiply_convert_fusion.5
  38.4 1.0 multiply_convert_fusion.3
  39.5 1.1 fusion.54
  40.5 75.2 %all-to-all-done = bf16[1,32,5,2,2,8,384]{6,5,4,2,3,0,1:T(8,128)(2,1)} async-done(((bf16[1,32,5,2,2,8,384]{6,5,4,2,3,0,1:T(8,128)(2,1)}), bf16[1,32,5,2,2,8,384]{6,5,4,2,3,0,1:T(8,128)(2,1)}, u32[]{:S(2)}, u32[]{:S(2)}) %all-to-all-start) | async-done | bytes 3932192 | tf_op jit(solution)/shard_map/all_to_all | solution.py:95
  115.7 6.0 %fusion.10 = bf16[5,2,2,384,256,1]{3,4,2,0,1,5:T(8,128)(2,1)S(1)} fusion(bf16[1,1,5,2,2,384,256]{5,6,4,2,3,1,0:T(8,128)(2,1)} %copy.90, f32[5,384,256]{1,2,0:T(8,128)S(1)} %copy-done.5, bf16[1,256,2,256]{1,3,0,2:T(8,128)(2,1)} %get-tuple-element.20, bf16[1,256,2,256]{1,3,0,2:T(8,128)(2,1)} %get-tuple-element.23, ...), kind=kOutput, calls=%fused_computation.14 | convolution fusion | flops 2022178816 | bytes 14286848 | tf_op jit(solution)/shard_map/pcerxzk,rzqj->pceqxkj/dot_general | solution.py:93
  121.7 2.2 fusion.9
  124.0 4.0 %copy.93 = bf16[1,1,5,2,2,256,384]{6,4,2,3,1,0,5:T(2,128)(2,1)S(1)} copy(bf16[1,1,5,2,2,256,384]{6,5,4,2,3,1,0:T(8,128)(2,1)S(1)} %fusion.9) | data formatting | bytes 7864320 | tf_op jit(solution)/shard_map/convert_element_type | solution.py:102
  128.0 100.2 %all_to_all.30 = bf16[1,1,5,2,2,256,384]{6,4,2,3,1,0,5:T(2,128)(2,1)S(1)} all-to-all(bf16[1,1,5,2,2,256,384]{6,4,2,3,1,0,5:T(2,128)(2,1)S(1)} %copy.93), channel_id=1, replica_groups=mesh['slab'=32,'coil'=8] {'slab'}, dimensions={5} | all-to-all | bytes 7864320 | tf_op jit(solution)/shard_map/all_to_all | solution.py:106
  228.2 4.7 %fusion.22 = f32[1,32,5,2,2,8,384]{6,1,5,4,2,3,0:T(8,128)S(1)} fusion(bf16[1,1,5,2,2,32,8,384]{7,4,2,3,6,5,1,0:T(2,128)(2,1)S(1)} %bitcast.183, bf16[1,384,2,384]{3,1,2,0:T(8,128)(2,1)S(1)} %copy-done.6, bf16[1,384,2,384]{3,1,2,0:T(8,128)(2,1)S(1)} %get-tuple-element.13), kind=kOutput, calls=%fused_computation.35 | convolution fusion | flops 3020488704 | bytes 12976128 | tf_op jit(solution)/shard_map/pcerxzy,ryqk->pceqxzk/dot_general | solution.py:52
  232.9 2.2 add_reduce_fusion
  235.3 3.1 collective-permute-start
  238.4 2.5 collective-permute-start.1
  240.9 2.5 collective-permute-done.1
  243.7 5.5 %collective-permute-start.3 = (bf16[1,10,2,10,384]{4,2,1,3,0:T(2,128)(2,1)S(1)}, bf16[1,10,2,10,384]{4,2,1,3,0:T(2,128)(2,1)S(1)}, u32[]{:S(2)}, u32[]{:S(2)}) collective-permute-start(bf16[1,10,2,10,384]{4,2,1,3,0:T(2,128)(2,1)S(1)} %pad_maximum_fusion.9), channel_id=1, source_target_pairs={{1,0},{2,1},{3,2},{4,3},{5,4},{6,5},{7,6},{9,8},{10,9},{11,10},{12... | collective-permute-start | bytes 460808 | tf_op jit(solution)/shard_map/ppermute | solution.py:21
  249.2 1.9 collective-permute-start.2
  251.8 5.9 %collective-permute-done.2 = bf16[1,10,2,10,384]{4,2,1,3,0:T(2,128)(2,1)S(1)} collective-permute-done((bf16[1,10,2,10,384]{4,2,1,3,0:T(2,128)(2,1)S(1)}, bf16[1,10,2,10,384]{4,2,1,3,0:T(2,128)(2,1)S(1)}, u32[]{:S(2)}, u32[]{:S(2)}) %collective-permute-start.2) | collective-permute-done | bytes 153632 | tf_op jit(solution)/shard_map/ppermute | solution.py:19
  258.9 1.0 pad.4.clone
  260.0 1.4 reshape.336
  262.5 7.2 %copy.100 = bf16[3,10,10,2,8,51]{1,4,3,5,2,0:T(8,128)(2,1)} copy(bf16[3,10,10,2,8,51]{5,4,3,2,1,0:T(8,128)(2,1)S(1)} %fusion.35) | data formatting | bytes 979200 | tf_op jit(solution)/shard_map/conv_general_dilated | solution.py:67
  269.8 7.9 %maximum_convert_fusion = bf16[1,8,16,49,64]{4,2,3,1,0:T(8,128)(2,1)S(1)} fusion(bf16[3,10,10,2,8,51]{1,4,3,5,2,0:T(8,128)(2,1)} %copy.100, f32[64]{0:T(128)S(1)} %copy-done.12, pred[16,49]{0,1:T(8,128)(4,1)S(1)} %copy-done.13, bf16[64,10,3,3,3]{0,4,3,2,1:T(4,128)(2,1)S(1)} %copy-done), kind=kOutput, calls=%fused_computation.34 | convolution fusion | flops 218365952 | bytes 1328016 | tf_op jit(solution)/shard_map/conv_general_dilated | solution.py:67
  278.9 4.1 %collective-permute-start.4 = (bf16[1,64,2,1,384]{4,2,1,3,0:T(2,128)(2,1)S(1)}, bf16[1,64,2,1,384]{4,2,1,3,0:T(2,128)(2,1)}, u32[]{:S(2)}, u32[]{:S(2)}) collective-permute-start(bf16[1,64,2,1,384]{4,2,1,3,0:T(2,128)(2,1)S(1)} %slice_bitcast_fusion.5), channel_id=1, source_target_pairs={{0,8},{8,16},{16,24},{24,32},{32,40},{40,48},{48,56},{56,64},{64,7... | collective-permute-start | bytes 294920 | tf_op jit(solution)/shard_map/ppermute | solution.py:19
  284.4 1.9 collective-permute-start.5
  286.4 1.0 copy.106
  287.5 0.9 copy.105
  288.4 2.3 collective-permute-done.5
  291.7 1.9 collective-permute-start.7
  293.7 3.4 collective-permute-start.6
  297.0 20.3 %collective-permute-done.7 = bf16[1,64,2,10,384]{4,1,3,2,0:T(8,128)(2,1)S(1)} collective-permute-done((bf16[1,64,2,10,384]{4,1,3,2,0:T(8,128)(2,1)S(1)}, bf16[1,64,2,10,384]{4,1,3,2,0:T(8,128)(2,1)S(1)}, u32[]{:S(2)}, u32[]{:S(2)}) %collective-permute-start.7) | collective-permute-done | bytes 983072 | tf_op jit(solution)/shard_map/ppermute | solution.py:21
  317.4 4.0 %collective-permute-done.6 = bf16[1,64,2,10,384]{4,1,3,2,0:T(8,128)(2,1)S(1)} collective-permute-done((bf16[1,64,2,10,384]{4,1,3,2,0:T(8,128)(2,1)S(1)}, bf16[1,64,2,10,384]{4,1,3,2,0:T(8,128)(2,1)S(1)}, u32[]{:S(2)}, u32[]{:S(2)}) %collective-permute-start.6) | collective-permute-done | bytes 983072 | tf_op jit(solution)/shard_map/ppermute | solution.py:19
  322.4 4.0 %pad.6.clone = bf16[3,64,10,2,392]{4,1,3,2,0:T(8,128)(2,1)} pad(bf16[3,64,10,2,384]{4,1,3,2,0:T(8,128)(2,1)S(1)} %copy.131, bf16[]{:T(256)} %constant.56), padding=0_0x0_0x0_0x0_0x1_7 | pad | bytes 5959682 | tf_op jit(solution)/shard_map/concatenate | solution.py:17
  326.4 12.5 %reshape.345 = bf16[3,64,10,2,8,49]{5,4,1,3,2,0:T(8,128)(2,1)} reshape(bf16[3,64,10,2,392]{4,1,3,2,0:T(8,128)(2,1)} %pad.6.clone) | data formatting | bytes 6021120 | tf_op jit(solution)/shard_map/conv_general_dilated | solution.py:67
  338.9 9.5 %slice.62 = bf16[3,64,10,2,7,2]{5,4,1,3,2,0:T(8,128)(2,1)} slice(bf16[3,64,10,2,8,49]{5,4,1,3,2,0:T(8,128)(2,1)} %reshape.345), slice={[0:3], [0:64], [0:10], [0:2], [1:8], [0:2]} | slice | bytes 215040 | tf_op jit(solution)/shard_map/conv_general_dilated | solution.py:67
  348.4 9.3 %fusion.1 = bf16[3,64,10,2,8,51]{5,4,1,3,2,0:T(8,128)(2,1)} fusion(bf16[3,64,10,2,7,2]{5,4,1,3,2,0:T(8,128)(2,1)} %slice.62, bf16[3,64,10,2,8,49]{5,4,1,3,2,0:T(8,128)(2,1)S(1)} %copy-done.2), kind=kLoop, calls=%fused_computation.2 | loop fusion | flops 9400320 | bytes 6251520 | tf_op jit(solution)/shard_map/conv_general_dilated | solution.py:67
  357.7 12.3 %copy.109 = bf16[3,64,10,2,8,51]{1,4,3,5,2,0:T(8,128)(2,1)} copy(bf16[3,64,10,2,8,51]{5,4,1,3,2,0:T(8,128)(2,1)} %fusion.1) | data formatting | bytes 6266880 | tf_op jit(solution)/shard_map/conv_general_dilated | solution.py:67
  370.0 14.5 %fusion.32 = f32[1,8,16,49,10]{4,2,3,1,0:T(8,128)S(1)} fusion(bf16[3,64,10,2,8,51]{1,4,3,5,2,0:T(8,128)(2,1)} %copy.109, pred[16,49]{0,1:T(8,128)(4,1)S(1)} %copy-done.13, bf16[10,64,3,3,3]{1,4,3,2,0:T(4,128)(2,1)S(1)} %copy-done.11), kind=kOutput, calls=%fused_computation.40 | convolution fusion | flops 216823040 | bytes 3419664 | tf_op jit(solution)/shard_map/conv_general_dilated | solution.py:67
  384.5 2.5 copy.111
  386.9 1.6 reshape.351
  (57 shorter events, 10.4 us)
Async XLA Ops:
  0.0 269.8 %copy-start = (bf16[64,10,3,3,3]{0,4,3,2,1:T(4,128)(2,1)S(1)}, bf16[64,10,3,3,3]{0,4,3,2,1:T(4,128)(2,1)}, u32[]{:S(2)}) copy-start(bf16[64,10,3,3,3]{0,4,3,2,1:T(4,128)(2,1)} %param.12) | copy-start | bytes 103684
  7.4 2.4 copy-start.3
  16.5 99.2 %all-to-all-start = ((bf16[1,32,5,2,2,8,384]{6,5,4,2,3,0,1:T(8,128)(2,1)}), bf16[1,32,5,2,2,8,384]{6,5,4,2,3,0,1:T(8,128)(2,1)}, u32[]{:S(2)}, u32[]{:S(2)}) async-start(bf16[1,32,5,2,2,8,384]{6,5,4,2,3,0,1:T(8,128)(2,1)} %copy.87), calls=%async_computation | async-start | bytes 7864320 | tf_op jit(solution)/shard_map/all_to_all | solution.py:95
  31.0 84.7 %copy-start.5 = (f32[5,384,256]{1,2,0:T(8,128)S(1)}, f32[5,384,256]{1,2,0:T(8,128)}, u32[]{:S(2)}) copy-start(f32[5,384,256]{1,2,0:T(8,128)} %copy.82) | copy-start | bytes 5898244
  115.7 6.0 %copy-start.8 = (bf16[1,256,2,256]{1,3,2,0:T(8,128)(2,1)S(1)}, bf16[1,256,2,256]{1,3,2,0:T(8,128)(2,1)}, u32[]{:S(2)}) copy-start(bf16[1,256,2,256]{1,3,2,0:T(8,128)(2,1)} %get-tuple-element.19) | copy-start | bytes 786436
  115.7 6.0 %copy-start.9 = (bf16[1,256,2,256]{1,3,2,0:T(8,128)(2,1)S(1)}, bf16[1,256,2,256]{1,3,2,0:T(8,128)(2,1)}, u32[]{:S(2)}) copy-start(bf16[1,256,2,256]{1,3,2,0:T(8,128)(2,1)} %get-tuple-element.24) | copy-start | bytes 786436
  128.0 100.2 %copy-start.6 = (bf16[1,384,2,384]{3,1,2,0:T(8,128)(2,1)S(1)}, bf16[1,384,2,384]{3,1,2,0:T(8,128)(2,1)}, u32[]{:S(2)}) copy-start(bf16[1,384,2,384]{3,1,2,0:T(8,128)(2,1)} %get-tuple-element.18) | copy-start | bytes 1769476
  228.2 4.7 %copy-start.4 = (f32[32,2,8,384]{3,0,2,1:T(8,128)S(1)}, f32[32,2,8,384]{3,0,2,1:T(8,128)}, u32[]{:S(2)}) copy-start(f32[32,2,8,384]{3,0,2,1:T(8,128)} %copy-done.3) | copy-start | bytes 2359300
  232.9 2.2 copy-start.7
  235.3 5.6 %collective-permute-start = (bf16[1,10,2,1,384]{4,2,1,3,0:T(2,128)(2,1)S(1)}, bf16[1,10,2,1,384]{4,2,1,3,0:T(2,128)(2,1)S(1)}, u32[]{:S(2)}, u32[]{:S(2)}) collective-permute-start(bf16[1,10,2,1,384]{4,2,1,3,0:T(2,128)(2,1)S(1)} %get-tuple-element.25), channel_id=1, source_target_pairs={{0,8},{8,16},{16,24},{24,32},{32,40},{40,48},{48,56},{56,64},{64,7... | collective-permute-start | bytes 46088 | tf_op jit(solution)/shard_map/ppermute | solution.py:19
  238.4 5.0 %collective-permute-start.1 = (bf16[1,10,2,1,384]{4,2,1,3,0:T(2,128)(2,1)S(1)}, bf16[1,10,2,1,384]{4,2,1,3,0:T(2,128)(2,1)S(1)}, u32[]{:S(2)}, u32[]{:S(2)}) collective-permute-start(bf16[1,10,2,1,384]{4,2,1,3,0:T(2,128)(2,1)S(1)} %get-tuple-element.26), channel_id=1, source_target_pairs={{8,0},{16,8},{24,16},{32,24},{40,32},{48,40},{56,48},{64,56},{72,6... | collective-permute-start | bytes 46088 | tf_op jit(solution)/shard_map/ppermute | solution.py:21
  243.7 8.2 %collective-permute-start.3 = (bf16[1,10,2,10,384]{4,2,1,3,0:T(2,128)(2,1)S(1)}, bf16[1,10,2,10,384]{4,2,1,3,0:T(2,128)(2,1)S(1)}, u32[]{:S(2)}, u32[]{:S(2)}) collective-permute-start(bf16[1,10,2,10,384]{4,2,1,3,0:T(2,128)(2,1)S(1)} %pad_maximum_fusion.9), channel_id=1, source_target_pairs={{1,0},{2,1},{3,2},{4,3},{5,4},{6,5},{7,6},{9,8},{10,9},{11,10},{12... | collective-permute-start | bytes 460808 | tf_op jit(solution)/shard_map/ppermute | solution.py:21
  249.2 8.6 %collective-permute-start.2 = (bf16[1,10,2,10,384]{4,2,1,3,0:T(2,128)(2,1)S(1)}, bf16[1,10,2,10,384]{4,2,1,3,0:T(2,128)(2,1)S(1)}, u32[]{:S(2)}, u32[]{:S(2)}) collective-permute-start(bf16[1,10,2,10,384]{4,2,1,3,0:T(2,128)(2,1)S(1)} %pad_maximum_fusion.9), channel_id=1, source_target_pairs={{0,1},{1,2},{2,3},{3,4},{4,5},{5,6},{6,7},{8,9},{9,10},{10,11},{11... | collective-permute-start | bytes 460808 | tf_op jit(solution)/shard_map/ppermute | solution.py:19
  262.5 7.3 %copy-start.12 = (f32[64]{0:T(128)S(1)}, f32[64]{0:T(128)}, u32[]{:S(2)}) copy-start(f32[64]{0:T(128)} %param.13) | copy-start | bytes 772
  262.5 7.3 %copy-start.13 = (pred[16,49]{0,1:T(8,128)(4,1)S(1)}, pred[16,49]{0,1:T(8,128)(4,1)}, u32[]{:S(2)}) copy-start(pred[16,49]{0,1:T(8,128)(4,1)} %constant.64) | copy-start | bytes 2356
  278.9 8.5 %collective-permute-start.4 = (bf16[1,64,2,1,384]{4,2,1,3,0:T(2,128)(2,1)S(1)}, bf16[1,64,2,1,384]{4,2,1,3,0:T(2,128)(2,1)}, u32[]{:S(2)}, u32[]{:S(2)}) collective-permute-start(bf16[1,64,2,1,384]{4,2,1,3,0:T(2,128)(2,1)S(1)} %slice_bitcast_fusion.5), channel_id=1, source_target_pairs={{0,8},{8,16},{16,24},{24,32},{32,40},{40,48},{48,56},{56,64},{64,7... | collective-permute-start | bytes 294920 | tf_op jit(solution)/shard_map/ppermute | solution.py:19
  284.4 6.2 %collective-permute-start.5 = (bf16[1,64,2,1,384]{4,2,1,3,0:T(2,128)(2,1)}, bf16[1,64,2,1,384]{4,2,1,3,0:T(2,128)(2,1)}, u32[]{:S(2)}, u32[]{:S(2)}) collective-permute-start(bf16[1,64,2,1,384]{4,2,1,3,0:T(2,128)(2,1)} %slice_bitcast_fusion.4), channel_id=1, source_target_pairs={{8,0},{16,8},{24,16},{32,24},{40,32},{48,40},{56,48},{64,56},{72,6... | collective-permute-start | bytes 294920 | tf_op jit(solution)/shard_map/ppermute | solution.py:21
  291.7 25.6 %collective-permute-start.7 = (bf16[1,64,2,10,384]{4,1,3,2,0:T(8,128)(2,1)S(1)}, bf16[1,64,2,10,384]{4,1,3,2,0:T(8,128)(2,1)S(1)}, u32[]{:S(2)}, u32[]{:S(2)}) collective-permute-start(bf16[1,64,2,10,384]{4,1,3,2,0:T(8,128)(2,1)S(1)} %pad_maximum_fusion), channel_id=1, source_target_pairs={{1,0},{2,1},{3,2},{4,3},{5,4},{6,5},{7,6},{9,8},{10,9},{11,10},{12... | collective-permute-start | bytes 2949128 | tf_op jit(solution)/shard_map/ppermute | solution.py:21
  293.7 27.7 %collective-permute-start.6 = (bf16[1,64,2,10,384]{4,1,3,2,0:T(8,128)(2,1)S(1)}, bf16[1,64,2,10,384]{4,1,3,2,0:T(8,128)(2,1)S(1)}, u32[]{:S(2)}, u32[]{:S(2)}) collective-permute-start(bf16[1,64,2,10,384]{4,1,3,2,0:T(8,128)(2,1)S(1)} %pad_maximum_fusion), channel_id=1, source_target_pairs={{0,1},{1,2},{2,3},{3,4},{4,5},{5,6},{6,7},{8,9},{9,10},{10,11},{11... | collective-permute-start | bytes 2949128 | tf_op jit(solution)/shard_map/ppermute | solution.py:19
  338.9 9.5 %copy-start.2 = (bf16[3,64,10,2,8,49]{5,4,1,3,2,0:T(8,128)(2,1)S(1)}, bf16[3,64,10,2,8,49]{5,4,1,3,2,0:T(8,128)(2,1)}, u32[]{:S(2)}) copy-start(bf16[3,64,10,2,8,49]{5,4,1,3,2,0:T(8,128)(2,1)} %reshape.345) | copy-start | bytes 9031684
  357.7 12.3 %copy-start.11 = (bf16[10,64,3,3,3]{1,4,3,2,0:T(4,128)(2,1)S(1)}, bf16[10,64,3,3,3]{1,4,3,2,0:T(4,128)(2,1)}, u32[]{:S(2)}) copy-start(bf16[10,64,3,3,3]{1,4,3,2,0:T(4,128)(2,1)} %param.14) | copy-start | bytes 103684
  370.0 19.4 %copy-start.1 = (bf16[64,10,3,3,3]{0,4,3,2,1:T(4,128)(2,1)S(1)}, bf16[64,10,3,3,3]{0,4,3,2,1:T(4,128)(2,1)}, u32[]{:S(2)}) copy-start(bf16[64,10,3,3,3]{0,4,3,2,1:T(4,128)(2,1)} %param.12) | copy-start | bytes 103684
  384.5 4.1 %copy-start.10 = (f32[10]{0:T(128)S(1)}, f32[10]{0:T(128)}, u32[]{:S(2)}) copy-start(f32[10]{0:T(128)} %param.15) | copy-start | bytes 124
where the time goes:
time: 397 us; the launch traced here: 390 us
  waiting for transfers between devices  111 us (28%)
  blocking collectives  100 us (25%)
  local copies, waits for them, and re-layouts  75.5 us (19%)
  matrix products  38.8 us (10%)
  starting transfers between devices  35.3 us (9%)
  other arithmetic  28.2 us (7%)
    all_to_all x1, blocking collectives, on_device(): lax.all_to_all(depth_back, 'slab', split_axis=5, concat_axis=1, tiled=True)  100 us
    all_to_all x1, waiting for transfers between devices, on_device(): lax.all_to_all(row_spectra, 'slab', split_axis=1, concat_axis=5, tiled=True)  75.2 us
    conv_general_dilated x8, local copies, waits for them, and re-layouts, convolve(): lax.conv_general_dilated(widened, weights, (1, 1, 1), 'VALID', dimension_...  47.3 us
    ppermute x4, waiting for transfers between devices, with_halo(): lax.ppermute(head, axis, [((i + 1) % count, i) for i in range(ends)])  25.9 us
    conv_general_dilated x2, matrix products, convolve(): lax.conv_general_dilated(widened, weights, (1, 1, 1), 'VALID', dimension_...  22.4 us
    ppermute x4, starting transfers between devices, with_halo(): lax.ppermute(tail, axis, [(i, (i + 1) % count) for i in range(ends)])  12.4 us
    ppermute x4, starting transfers between devices, with_halo(): lax.ppermute(head, axis, [((i + 1) % count, i) for i in range(ends)])  11.9 us
    all_to_all x1, starting transfers between devices, on_device(): lax.all_to_all(row_spectra, 'slab', split_axis=1, concat_axis=5, tiled=True)  11 us
  transfers between devices with their start and end apart: 9, of which 7 were waited for; matrix products, arithmetic and copies ran while one was open for 4% of the time, Pallas kernels for 0%

commit v1 on v0

v1 whole, which is shorter than its diff:
```python
import functools
import math

import jax
import jax.numpy as jnp
import numpy as np
from jax import lax
from jax.experimental import pallas as pl
from jax.experimental.pallas import tpu as pltpu
from jax.sharding import PartitionSpec as P

MESH = pl.DeviceIdType.MESH
BF = jnp.bfloat16
F32 = jnp.float32
NY, NZ, E, FEAT = 384, 256, 5, 64
SLABS, PHASES = 32, 8


def dft_parts(length):
    indices = np.arange(length, dtype=np.int64)
    wrapped = indices[:, None] * indices[None, :] % length
    angles = wrapped.astype(np.float32) * np.float32(2.0 * math.pi / length)
    factor = np.float32(1.0 / math.sqrt(length))
    return np.cos(angles) * factor, np.sin(angles) * factor


def tables():
    cy, sy = dft_parts(NY)
    cz, sz = dft_parts(NZ)
    wy = np.block([[cy, sy], [-sy, cy]]).astype(jnp.bfloat16)
    wz = np.block([[cz, -sz], [sz, cz]]).astype(jnp.bfloat16)
    return wy, wz


def place():
    s = lax.axis_index("slab")
    p = lax.axis_index("coil")
    return s, p, s // 16, (s // 2) % 8, s % 2


def slab_of(xh, z, c):
    return xh * 16 + z * 2 + c


def rcopy(src, dst, ssem, rsem, s, p):
    return pltpu.make_async_remote_copy(
        src_ref=src,
        dst_ref=dst,
        send_sem=ssem,
        recv_sem=rsem,
        device_id={"slab": s, "coil": p},
        device_id_type=MESH,
    )


def gather_kernel(img, maps, G, M, xs, xr, rs, rr, cs, cr, s1s, s1r, s2s, s2r, ls):
    s, p, xh, z, c = place()
    sib = slab_of(xh, z, 1 - c)
    xp = slab_of(1 - xh, z, c)
    ring = [slab_of(xh, (z + 1) % 8, c), slab_of(xh, (z + 7) % 8, c)]
    barrier = pltpu.get_barrier_semaphore()

    def greet(a, b):
        pl.semaphore_signal(
            barrier, inc=1, device_id={"slab": a, "coil": b}, device_id_type=MESH
        )

    for a in (sib, xp, ring[0], ring[1]):
        greet(a, p)
    for q in range(1, 8):
        greet(s, (p + q) % 8)
    for j in range(4):
        delta = 4 * p + j

        @pl.when(delta != 0)
        def _():
            greet((s + 32 - delta) % 32, p)

    pl.semaphore_wait(barrier, 15 - jnp.where(p == 0, 1, 0))

    def slot(col, dz):
        return slab_of((xh + col) % 2, (z + dz) % 8, c)

    def ring_copy(src, col, d, t, k):
        if t == 4:
            src, dst = src.at[:, d], G.at[:, k, d]
        else:
            dst = G.at[:, k]
        return rcopy(src, dst, rs.at[col, d, t - 1], rr.at[col, d, t - 1], ring[d], p)

    def core_copy(src, col, dz, k):
        return rcopy(src, G.at[:, k], cs.at[col, dz], cr.at[col, dz], sib, p)

    sends = []

    def go(copy):
        copy.start()
        sends.append(copy)

    go(rcopy(img, G.at[:, s], xs, xr, xp, p))
    for d in range(2):
        go(ring_copy(img, 0, d, 1, s))
    own = pltpu.make_async_copy(img, G.at[:, s], ls.at[0])
    own.start()
    for j in range(4):
        delta = 4 * p + j
        far = (s + delta) % 32

        @pl.when(delta != 0)
        def _():
            rcopy(maps.at[far], M.at[s], s1s.at[j], s1r.at[j], far, p).start()

        @pl.when(delta == 0)
        def _():
            pltpu.make_async_copy(maps.at[s], M.at[s], ls.at[1]).start()

    go(core_copy(img, 0, 0, s))
    rcopy(img, G.at[:, xp], xs, xr, xp, p).wait_recv()
    for d in range(2):
        go(ring_copy(G.at[:, xp], 1, d, 1, xp))
    go(core_copy(G.at[:, xp], 1, 0, xp))
    for j in range(4):
        delta = 4 * p + j
        near = (s + 32 - delta) % 32

        @pl.when(delta != 0)
        def _():
            rcopy(maps.at[s], M.at[near], s1s.at[j], s1r.at[j], near, p).wait_recv()

        @pl.when(delta == 0)
        def _():
            pltpu.make_async_copy(maps.at[s], M.at[s], ls.at[1]).wait()

        for q in range(1, 8):
            go(rcopy(M.at[near], M.at[near], s2s.at[j, q - 1], s2r.at[j, q - 1], s, (p + q) % 8))
    for t in range(1, 5):
        for col in range(2):
            for d in range(2):
                dz = (8 - t) if d == 0 else t
                k = slot(col, dz)
                here = G.at[:, k]
                ring_copy(here, col, d, t, k).wait_recv()
                if t < 4:
                    go(ring_copy(here, col, d, t + 1, k))
                    go(core_copy(here, col, dz, k))
            if t == 4:
                k = slot(col, 4)
                go(core_copy(G.at[:, k], col, 4, k))
    for q in range(1, 8):
        for j in range(4):
            near = (s + 64 - (4 * ((p + 8 - q) % 8) + j)) % 32
            rcopy(M.at[near], M.at[near], s2s.at[j, q - 1], s2r.at[j, q - 1], s, p).wait_recv()
    for col in range(2):
        for dz in range(8):
            k = slab_of((xh + col) % 2, (z + dz) % 8, 1 - c)
            core_copy(G.at[:, k], col, dz, k).wait_recv()
    own.wait()
    for copy in sends:
        copy.wait_send()
    for j in range(4):
        delta = 4 * p + j
        far = (s + delta) % 32

        @pl.when(delta != 0)
        def _():
            rcopy(maps.at[far], M.at[s], s1s.at[j], s1r.at[j], far, p).wait_send()


def gather(img, maps):
    any_spec = pl.BlockSpec(memory_space=pl.ANY)
    sem = pltpu.SemaphoreType.DMA
    return pl.pallas_call(
        gather_kernel,
        out_shape=(
            jax.ShapeDtypeStruct((E, SLABS, 2, 2, 8, NY), BF),
            jax.ShapeDtypeStruct((SLABS, 2, 2, 8, NY), BF),
        ),
        in_specs=[any_spec] * 2,
        out_specs=(any_spec, any_spec),
        scratch_shapes=[
            sem,
            sem,
            sem((2, 2, 4)),
            sem((2, 2, 4)),
            sem((2, 8)),
            sem((2, 8)),
            sem((4,)),
            sem((4,)),
            sem((4, 7)),
            sem((4, 7)),
            sem((2,)),
        ],
        compiler_params=pltpu.CompilerParams(collective_id=0, has_side_effects=True),
        name="gather",
    )(img, maps)


NT = (((1,), (1,)), ((), ()))
NN = (((1,), (0,)), ((), ()))


def mm(a, b, dims):
    return lax.dot_general(a, b, dims, preferred_element_type=F32)


def dft_kernel(g_ref, m_ref, meas_ref, samp_ref, wy_ref, wz_ref, out_ref):
    mask = samp_ref[0].astype(F32)
    for x in range(2):
        wide = lambda v: v.astype(F32).reshape(NZ, NY)
        mr, mi = wide(m_ref[:, 0, x]), wide(m_ref[:, 1, x])
        ir, ii = wide(g_ref[0, :, 0, x]), wide(g_ref[0, :, 1, x])
        pr = (mr * ir - mi * ii).astype(BF)
        pi = (mr * ii + mi * ir).astype(BF)
        r = mm(wy_ref[...], jnp.concatenate([pr, pi], axis=1), NT).astype(BF)
        rc = jnp.concatenate([r[:NY], r[NY:]], axis=1)
        sp = mm(rc, wz_ref[...], NN)
        dr = (mask * (sp[:, :NZ] - meas_ref[0, 0, x].astype(F32))).astype(BF)
        di = (mask * (sp[:, NZ:] - meas_ref[0, 1, x].astype(F32))).astype(BF)
        b = mm(wz_ref[...], jnp.concatenate([dr, di], axis=1), NT).astype(BF)
        bc = jnp.concatenate([b[:NZ], b[NZ:]], axis=1)
        im = mm(bc, wy_ref[...], NN)
        br, bi = im[:, :NY], im[:, NY:]
        out_ref[0, :, 0, x] = (mr * br + mi * bi).reshape(SLABS, 8, NY).astype(BF)
        out_ref[0, :, 1, x] = (mr * bi - mi * br).reshape(SLABS, 8, NY).astype(BF)


def dft(G, M, meas, samp, wy, wz):
    whole = lambda shape: pl.BlockSpec(shape, lambda e: (0,) * len(shape))
    per_e = lambda shape: pl.BlockSpec((1,) + shape, lambda e: (e,) + (0,) * len(shape))
    return pl.pallas_call(
        dft_kernel,
        grid=(E,),
        out_shape=jax.ShapeDtypeStruct((E, SLABS, 2, 2, 8, NY), BF),
        in_specs=[
            per_e((SLABS, 2, 2, 8, NY)),
            whole((SLABS, 2, 2, 8, NY)),
            per_e((2, 2, NY, NZ)),
            per_e((NY, NZ)),
            whole((2 * NY, 2 * NY)),
            whole((2 * NZ, 2 * NZ)),
        ],
        out_specs=per_e((SLABS, 2, 2, 8, NY)),
        compiler_params=pltpu.CompilerParams(vmem_limit_bytes=60 * 1024 * 1024),
        name="dft",
    )(G, M, meas, samp, wy, wz)


def reduce_kernel(
    gd, img, U, H, sibbuf, S, rbuf, sbuf, xsb, xrb, esc, esend, erecv,
    cs, cr, rs, rr, xs, xr, es, er, us, ur, hs, hr,
):
    s, p, xh, z, c = place()
    sib = slab_of(xh, z, 1 - c)
    xp = slab_of(1 - xh, z, c)
    ring = [slab_of(xh, (z + 1) % 8, c), slab_of(xh, (z + 7) % 8, c)]
    has_up, has_down = s > 0, s < SLABS - 1
    has_before, has_after = p > 0, p < PHASES - 1
    barrier = pltpu.get_barrier_semaphore()

    def greet(a, b):
        pl.semaphore_signal(
            barrier, inc=1, device_id={"slab": a, "coil": b}, device_id_type=MESH
        )

    for a in (sib, xp, ring[0], ring[1]):
        greet(a, p)
    pl.when(has_up)(lambda: greet(s - 1, p))
    pl.when(has_down)(lambda: greet(s + 1, p))
    pl.when(has_before)(lambda: greet(s, p - 1))
    pl.when(has_after)(lambda: greet(s, p + 1))
    one = lambda cond: jnp.where(cond, 1, 0)
    pl.semaphore_wait(
        barrier, 4 + one(has_up) + one(has_down) + one(has_before) + one(has_after)
    )

    def sib_copy(e):
        return rcopy(gd.at[e, :, :, 1 - c], sibbuf.at[e], cs.at[e], cr.at[e], sib, p)

    def ring_copy(h, e, col, d):
        src, dst = sbuf.at[h, col, d, e], rbuf.at[h, col, d, e]
        if h == 0:
            src, dst = src.at[d], dst.at[d]
        return rcopy(src, dst, rs.at[h, col, d, e], rr.at[h, col, d, e], ring[d], p)

    def x_copy(e):
        return rcopy(xsb.at[e], xrb.at[e], xs.at[e], xr.at[e], xp, p)

    @pl.loop(0, E)
    def _(e):
        sib_copy(e).start()

    @pl.loop(0, E)
    def _(e):
        sib_copy(e).wait_recv()

        @pl.loop(0, 8)
        def _(zz):
            S[e, :, zz] = gd[e, :, zz, c].astype(F32) + sibbuf[e, :, zz].astype(F32)

        for col in range(2):
            for d in range(2):
                sbuf[0, col, d, e, d] = S[e, (xh + col) % 2, (z + 4) % 8, d].astype(BF)
                ring_copy(0, e, col, d).start()

    for h in range(1, 4):

        @pl.loop(0, E)
        def _(e):
            for col in range(2):
                for d in range(2):
                    ring_copy(h - 1, e, col, d).wait_recv()
                    k = 4 - h
                    tz = (z + k) % 8 if d == 0 else (z + 8 - k) % 8
                    lane = (xh + col) % 2
                    if h == 1:
                        v = S[e, lane, tz, d] + rbuf[0, col, d, e, d].astype(F32)
                        sbuf[1, col, d, e, d] = v.astype(BF)
                        sbuf[1, col, d, e, 1 - d] = S[e, lane, tz, 1 - d].astype(BF)
                    else:
                        v = S[e, lane, tz] + rbuf[h - 1, col, d, e].astype(F32)
                        sbuf[h, col, d, e] = v.astype(BF)
                    ring_copy(h, e, col, d).start()

    @pl.loop(0, E)
    def _(e):
        for col in (1, 0):
            for d in range(2):
                ring_copy(3, e, col, d).wait_recv()
            lane = (xh + col) % 2
            v = S[e, lane, z] + rbuf[3, col, 0, e].astype(F32) + rbuf[3, col, 1, e].astype(F32)
            if col == 1:
                xsb[e] = v.astype(BF)
                x_copy(e).start()
            else:
                S[e, lane, z] = v

    @pl.loop(0, E)
    def _(e):
        x_copy(e).wait_recv()
        g = S[e, xh, z] + xrb[e].astype(F32)
        u = (img[e].astype(F32) - g).astype(BF)
        U[2, e] = u
        v = u.astype(F32)
        for x in range(2):
            esc[e, :, 4 * x : 4 * x + 2] = v[:, x, 6:8]
            esc[e, :, 4 * x + 2 : 4 * x + 4] = v[:, x, 0:2]
        esend[e] = esc[e].astype(BF)

    def u_copy(i):
        src, dst, q = ((2, 1, p + 1), (2, 3, p - 1), (1, 0, p + 1), (3, 4, p - 1))[i]
        return rcopy(U.at[src], U.at[dst], us.at[i], ur.at[i], s, q)

    def h_copy(i):
        src, dst, q = ((2, 1, p + 1), (2, 3, p - 1), (1, 0, p + 1), (3, 4, p - 1))[i]
        return rcopy(H.at[src], H.at[dst], hs.at[i], hr.at[i], s, q)

    def e_copy(i):
        return rcopy(esend, erecv.at[i], es.at[i], er.at[i], (s + 1, s - 1)[i], p)

    through_up = jnp.logical_and(has_before, has_after)
    pl.when(has_down)(lambda: e_copy(0).start())
    pl.when(has_up)(lambda: e_copy(1).start())
    pl.when(has_after)(lambda: u_copy(0).start())
    pl.when(has_before)(lambda: u_copy(1).start())
    pl.when(has_up)(lambda: e_copy(0).wait_recv())
    pl.when(has_down)(lambda: e_copy(1).wait_recv())
    row = lax.broadcasted_iota(jnp.int32, (2, 8, NY), 1) % 4
    for e in range(E):
        up = jnp.where(has_up, erecv[0, e].astype(F32), 0.0)
        down = jnp.where(has_down, erecv[1, e].astype(F32), 0.0)
        H[2, e] = jnp.where(row < 2, up, down).astype(BF)
    pl.when(has_after)(lambda: h_copy(0).start())
    pl.when(has_before)(lambda: h_copy(1).start())
    for copy in (u_copy, h_copy):
        pl.when(has_before)(lambda: copy(0).wait_recv())
        pl.when(through_up)(lambda: copy(2).start())
        pl.when(has_after)(lambda: copy(1).wait_recv())
        pl.when(through_up)(lambda: copy(3).start())
    for copy in (u_copy, h_copy):
        pl.when(p > 1)(lambda: copy(2).wait_recv())
        pl.when(p < PHASES - 2)(lambda: copy(3).wait_recv())

    @pl.loop(0, E)
    def _(e):
        sib_copy(e).wait_send()
        x_copy(e).wait_send()
        for h in range(4):
            for col in range(2):
                for d in range(2):
                    ring_copy(h, e, col, d).wait_send()

    pl.when(has_down)(lambda: e_copy(0).wait_send())
    pl.when(has_up)(lambda: e_copy(1).wait_send())
    for copy in (u_copy, h_copy):
        pl.when(has_after)(lambda: copy(0).wait_send())
        pl.when(has_before)(lambda: copy(1).wait_send())
        pl.when(through_up)(lambda: copy(2).wait_send())
        pl.when(through_up)(lambda: copy(3).wait_send())


def reduce(gd, img):
    sem = pltpu.SemaphoreType.DMA
    vm = pl.BlockSpec(memory_space=pltpu.VMEM)
    return pl.pallas_call(
        reduce_kernel,
        out_shape=(
            jax.ShapeDtypeStruct((5, E, 2, 2, 8, NY), BF),
            jax.ShapeDtypeStruct((5, E, 2, 8, NY), BF),
        ),
        in_specs=[vm, vm],
        out_specs=(vm, vm),
        scratch_shapes=[
            pltpu.VMEM((E, 2, 8, 2, 2, 8, NY), BF),
            pltpu.VMEM((E, 2, 8, 2, 2, 8, NY), F32),
            pltpu.VMEM((4, 2, 2, E, 2, 2, 8, NY), BF),
            pltpu.VMEM((4, 2, 2, E, 2, 2, 8, NY), BF),
            pltpu.VMEM((E, 2, 2, 8, NY), BF),
            pltpu.VMEM((E, 2, 2, 8, NY), BF),
            pltpu.VMEM((E, 2, 8, NY), F32),
            pltpu.VMEM((E, 2, 8, NY), BF),
            pltpu.VMEM((2, E, 2, 8, NY), BF),
            sem((E,)),
            sem((E,)),
            sem((4, 2, 2, E)),
            sem((4, 2, 2, E)),
            sem((E,)),
            sem((E,)),
            sem((2,)),
            sem((2,)),
            sem((4,)),
            sem((4,)),
            sem((4,)),
            sem((4,)),
        ],
        compiler_params=pltpu.CompilerParams(
            collective_id=1, has_side_effects=True, vmem_limit_bytes=60 * 1024 * 1024
        ),
        name="reduce",
    )(gd, img)


K1 = 9 * 10 * 16
K1P = 1536
K2 = 3 * 10 * FEAT


def conv_kernel(U, H, w1_ref, b1_ref, w2_ref, b2_ref, out_ref, W1, W2, col, V, hid, osc):
    s = lax.axis_index("slab")
    p = lax.axis_index("coil")
    base = w1_ref[...].astype(F32)
    for zo in range(10):
        turned = base if zo == 0 else pltpu.roll(base, zo, 1)
        W1[zo * FEAT : (zo + 1) * FEAT, :] = turned[:, :K1].astype(BF)
    for d in range(3):
        base2 = w2_ref[d].astype(F32)
        for zz in range(8):
            turned = base2 if zz == 0 else pltpu.roll(base2, zz * FEAT, 1)
            W2[d * 128 + zz * 16 : d * 128 + zz * 16 + 16, :] = turned.astype(BF)
    lane = lax.broadcasted_iota(jnp.int32, (160, NY), 1)
    col[...] = jnp.zeros_like(col)
    for q in range(5):
        there = jnp.logical_and(p + q >= 2, p + q < PHASES + 2)
        for x in range(2):
            halo = H[q].reshape(10, 8, NY).astype(F32)
            col[:, 2:10] = U[q, :, :, x].reshape(10, 8, NY).astype(F32)
            col[:, 0:2] = halo[:, 4 * x : 4 * x + 2]
            col[:, 10:12] = halo[:, 4 * x + 2 : 4 * x + 4]
            v = jnp.where(there, col[...].reshape(160, NY), 0.0)
            back = jnp.where(lane == 0, 0.0, pltpu.roll(v, 1, 1))
            ahead = jnp.where(lane == NY - 1, 0.0, pltpu.roll(v, NY - 1, 1))
            for d, part in enumerate((back, v, ahead)):
                first = (q * 3 + d) * 160
                V[first : first + 160, x * NY : (x + 1) * NY] = part.astype(BF)
    rows = lax.broadcasted_iota(jnp.int32, (640, 2 * NY), 0)
    lowest = jnp.where(s == 0, FEAT, 0)
    highest = jnp.where(s == SLABS - 1, 9 * FEAT, 10 * FEAT)
    for t in range(3):
        there = jnp.logical_and(p + t >= 1, p + t < PHASES + 1)
        h = mm(W1[...], V[t * 480 : t * 480 + K1, :], NN) + b1_ref[...]
        keep = jnp.logical_and(jnp.logical_and(rows >= lowest, rows < highest), there)
        hid[t * 640 : (t + 1) * 640, :] = jnp.where(keep, jnp.maximum(h, 0.0), 0.0).astype(BF)
    o = mm(W2[...], hid[...], NN)
    lane2 = lax.broadcasted_iota(jnp.int32, (128, 2 * NY), 1) % NY
    total = (
        o[128:256]
        + jnp.where(lane2 == 0, 0.0, pltpu.roll(o[:128], 1, 1))
        + jnp.where(lane2 == NY - 1, 0.0, pltpu.roll(o[256:], 2 * NY - 1, 1))
    )
    for k in range(6):
        osc[k] = total[:, k * 128 : (k + 1) * 128]
    for i in range(10):
        for x in range(2):
            second = jnp.concatenate(
                [osc[3 * x + k, pl.ds(i, 8, stride=16), :] for k in range(3)], axis=1
            )
            v = U[2, i // 2, i % 2, x].astype(F32) + second + b2_ref[i]
            out_ref[i // 2, i % 2, x] = v.astype(BF)


def conv(U, H, first_weight, first_bias, second_weight, second_bias):
    w1 = first_weight.transpose(0, 2, 4, 1, 3)
    w1 = jnp.pad(w1, ((0, 0),) * 4 + ((0, 13),)).reshape(FEAT, K1)
    w1 = jnp.pad(w1, ((0, 0), (0, K1P - K1)))
    w2 = second_weight.transpose(4, 0, 2, 3, 1)
    w2 = jnp.pad(w2, ((0, 0), (0, 6), (0, 0), (0, 7), (0, 0))).reshape(3, 16, K2)
    b1 = jnp.tile(first_bias, 10)[:, None]
    vm = pl.BlockSpec(memory_space=pltpu.VMEM)
    return pl.pallas_call(
        conv_kernel,
        out_shape=jax.ShapeDtypeStruct((E, 2, 2, 8, NY), BF),
        in_specs=[vm, vm, vm, vm, vm, pl.BlockSpec(memory_space=pltpu.SMEM)],
        out_specs=vm,
        scratch_shapes=[
            pltpu.VMEM((640, K1), BF),
            pltpu.VMEM((384, K2), BF),
            pltpu.VMEM((10, 16, NY), F32),
            pltpu.VMEM((2400, 2 * NY), BF),
            pltpu.VMEM((1920, 2 * NY), BF),
            pltpu.VMEM((6, 128, 128), F32),
        ],
        compiler_params=pltpu.CompilerParams(vmem_limit_bytes=60 * 1024 * 1024),
        name="conv",
    )(U, H, w1, b1, w2, second_bias)


def on_device(
    current_image,
    coil_maps,
    measured,
    sampling,
    first_weight,
    first_bias,
    second_weight,
    second_bias,
):
    wy, wz = tables()
    img = current_image[0]
    G, M = gather(img, coil_maps)
    gd = dft(G, M, measured[0, 0], sampling[0], jnp.asarray(wy), jnp.asarray(wz))
    U, H = reduce(gd.reshape(E, 2, 8, 2, 2, 2, 8, NY), img)
    out = conv(U, H, first_weight, first_bias, second_weight, second_bias)
    return out[None]


def solution(mesh):
    in_specs = (
        P("coil", None, None, None, "slab", None),
        P(None, None, None, "slab", None),
        P("coil", "slab", None, None, None, None, None),
        P("coil", None, None, None),
        P(),
        P(),
        P(),
        P(),
    )
    out_specs = P("coil", None, None, None, "slab", None)
    return jax.shard_map(
        on_device, mesh=mesh, in_specs=in_specs, out_specs=out_specs, check_vma=False
    )
```

time: 397 us -> 120 us (0.30)
  the two profiles are of different devices: /device:TPU:35 before, /device:TPU:24 now
where the time goes in v1:
time: 120 us; the launch traced here: 118 us
  Pallas kernels  114 us (95%)
  local copies, waits for them, and re-layouts  3.14 us (3%)
    pallas_call x1, Pallas kernels, reduce(): pl.pallas_call(reduce_kernel, out_shape=(jax.ShapeDtypeStruct((5, E, 2, 2...  48.8 us
    pallas_call x1, Pallas kernels, gather(): pl.pallas_call(gather_kernel, out_shape=(jax.ShapeDtypeStruct((E, SLABS,...  35.9 us
    pallas_call x1, Pallas kernels, dft(): pl.pallas_call(dft_kernel, grid=(E,), out_shape=jax.ShapeDtypeStruct((E,...  20.9 us
    pallas_call x1, Pallas kernels, conv(): pl.pallas_call(conv_kernel, out_shape=jax.ShapeDtypeStruct((E, 2, 2, 8, N...  8.85 us

profile of v1, /device:TPU:24, one launch (start us, length us, event | category | flops | bytes accessed | tf_op | source)
XLA Modules:
  0.0 117.6 jit_solution(696141799329575145)
XLA Ops:
  0.0 35.9 %gather.1 = (bf16[5,32,2,2,8,384]{5,4,3,2,1,0:T(8,128)(2,1)}, bf16[32,2,2,8,384]{4,3,2,1,0:T(8,128)(2,1)}) custom-call(bf16[5,2,2,8,384]{4,3,2,1,0:T(8,128)(2,1)} %bitcast.12, bf16[32,2,2,8,384]{4,3,2,1,0:T(8,128)(2,1)} %maps.1), custom_call_target="tpu_custom_call" | custom-call | tf_op jit(solution)/shard_map/gather/pallas_call | solution.py:172
  35.9 20.9 %dft.1 = bf16[5,32,2,2,8,384]{5,4,3,2,1,0:T(8,128)(2,1)} custom-call(bf16[5,32,2,2,8,384]{5,4,3,2,1,0:T(8,128)(2,1)} %get-tuple-element.9.g_ref, bf16[32,2,2,8,384]{4,3,2,1,0:T(8,128)(2,1)} %get-tuple-element.10.m_ref, bf16[5,2,2,384,256]{4,3,2,1,0:T(8,128)(2,1)} %bitcast.9, s32[5,384,256]{2,1,0:T(8,128)} %bitcast.10, ...), custom_call_target="tpu_custom_call" | custom-call | tf_op jit(solution)/shard_map/dft/pallas_call | solution.py:230
  56.8 0.0 copy-start
  56.8 0.0 copy-start.1
  56.8 0.0 copy-start.2
  56.8 48.8 %reduce.1 = (bf16[5,5,2,2,8,384]{5,4,3,2,1,0:T(8,128)(2,1)}, bf16[5,5,2,8,384]{4,3,2,1,0:T(8,128)(2,1)}) custom-call(bf16[5,2,8,2,2,2,8,384]{7,6,5,4,3,2,1,0:T(8,128)(2,1)} %bitcast.8, bf16[5,2,2,8,384]{4,3,2,1,0:T(8,128)(2,1)} %bitcast.13), custom_call_target="tpu_custom_call" | custom-call | tf_op jit(solution)/shard_map/reduce/pallas_call | solution.py:404
  105.6 0.0 copy-done
  105.6 0.1 pad.14.clone
  105.7 1.0 reshape.12.w2_ref
  106.8 0.0 copy-done.1
  106.8 0.1 pad.12.clone
  106.9 0.2 copy.14
  107.1 0.7 pad.13.w1_ref
  107.8 0.0 copy-done.2
  107.8 1.0 broadcast_in_dim_tile.4.b1_ref
  108.8 8.8 %conv.1 = bf16[5,2,2,8,384]{4,3,2,1,0:T(8,128)(2,1)} custom-call(bf16[5,5,2,2,8,384]{5,4,3,2,1,0:T(8,128)(2,1)} %get-tuple-element.11.U, bf16[5,5,2,8,384]{4,3,2,1,0:T(8,128)(2,1)} %get-tuple-element.12.H, bf16[64,1536]{1,0:T(8,128)(2,1)} %pad.13.w1_ref, f32[640,1]{1,0:T(8,128)} %broadcast_in_dim_tile.4.b1_ref, bf16[3,16,1920]{2,1,0:T(8,128)(2,1)} %reshape.12.w2_ref, ...), custom_call_target="tpu_custom_call" | custom-call | tf_op jit(solution)/shard_map/conv/pallas_call | solution.py:508
  (3 shorter events, 0.1 us)
Async XLA Ops:
  56.8 48.8 %copy-start = (bf16[10,64,3,3,3]{1,4,3,2,0:T(4,128)(2,1)S(1)}, bf16[10,64,3,3,3]{1,4,3,2,0:T(4,128)(2,1)}, u32[]{:S(2)}) copy-start(bf16[10,64,3,3,3]{1,4,3,2,0:T(4,128)(2,1)} %param.16) | copy-start | bytes 103684
  56.8 50.0 %copy-start.1 = (bf16[64,10,3,3,3]{0,4,3,2,1:T(4,128)(2,1)S(1)}, bf16[64,10,3,3,3]{0,4,3,2,1:T(4,128)(2,1)}, u32[]{:S(2)}) copy-start(bf16[64,10,3,3,3]{0,4,3,2,1:T(4,128)(2,1)} %param.14) | copy-start | bytes 103684
  56.8 51.0 %copy-start.2 = (f32[64]{0:T(128)S(1)}, f32[64]{0:T(128)}, u32[]{:S(2)}) copy-start(f32[64]{0:T(128)} %param.15) | copy-start | bytes 772

commit v2 on v0

v2 whole, which is shorter than its diff:
```python
import functools
import math

import jax
import jax.numpy as jnp
import numpy as np
from jax import lax
from jax.experimental import pallas as pl
from jax.experimental.pallas import tpu as pltpu
from jax.sharding import PartitionSpec as P

MESH = pl.DeviceIdType.MESH
BF = jnp.bfloat16
F32 = jnp.float32
NY, NZ, E, FEAT = 384, 256, 5, 64
SLABS, PHASES = 32, 8
NT = (((1,), (1,)), ((), ()))
NN = (((1,), (0,)), ((), ()))
OFFSETS = (1, -1, 2, -2)
SHARE = (4, 1, 7, 3, 5, 2, 6)
KA, KB = 9 * 8 * 16, 9 * 2 * 16
K2 = 3 * 10 * FEAT


def dft_parts(length):
    indices = np.arange(length, dtype=np.int64)
    wrapped = indices[:, None] * indices[None, :] % length
    angles = wrapped.astype(np.float32) * np.float32(2.0 * math.pi / length)
    factor = np.float32(1.0 / math.sqrt(length))
    return np.cos(angles) * factor, np.sin(angles) * factor


def tables():
    cy, sy = dft_parts(NY)
    cz, sz = dft_parts(NZ)
    wy = np.stack([cy, sy]).astype(jnp.bfloat16)
    wz = np.stack([cz, sz]).astype(jnp.bfloat16)
    return wy, wz


def place():
    s = lax.axis_index("slab")
    p = lax.axis_index("coil")
    return s, p, s // 16, (s // 2) % 8, s % 2


def slab_of(xh, z, c):
    return xh * 16 + z * 2 + c


def rcopy(src, dst, ssem, rsem, s, p):
    return pltpu.make_async_remote_copy(
        src_ref=src,
        dst_ref=dst,
        send_sem=ssem,
        recv_sem=rsem,
        device_id={"slab": s, "coil": p},
        device_id_type=MESH,
    )


def mm(a, b, dims):
    return lax.dot_general(a, b, dims, preferred_element_type=F32)


STAGE = {1: ["m1"], 2: [("g", 0, 0, 1, 2)], 3: [("g", 0, 1, 1, 3)], 4: [("far", 0, 1)]}


class Plan:
    LINKS = {"z0": (0.5, 2.1), "z1": (0.5, 2.1), "x": (0.5, 3.0), "c": (0.05, 1.6),
             "y": (1.5, 3.2), "e": (0.5, 6.0), "m1": (0.5, 4.0), "m2": (0.3, 3.0)}

    def __init__(self):
        self.tasks = []

    def add(self, name, fn, after=(), needs=(), sends=(), cost=0.05, rank=0):
        self.tasks.append((name, fn, tuple(after), tuple(needs), tuple(sends), cost, rank))

    def run(self):
        now, done, arrive, free = 0.0, {}, {}, {}
        left = list(self.tasks)
        while left:
            best = None
            for i, (name, _, after, needs, _, _, rank) in enumerate(left):
                if any(a not in done for a in after) or any(m not in arrive for m in needs):
                    continue
                ready = max([0.0] + [arrive[m] for m in needs])
                key = (max(ready, now), rank, i)
                if best is None or key < best[0]:
                    best = (key, i)
            name, fn, _, _, sends, cost, _ = left.pop(best[1])
            now = best[0][0] + cost
            for message, link, size in sends:
                rate, lag = self.LINKS[link]
                free[link] = max(free.get(link, 0.0), now) + rate * size
                arrive[message] = free[link] + lag
            done[name] = now
            fn()
        return now


def kernel(
    img_h, maps, meas_h, samp_h, wy_h, wz_h, w1_ref, b1_ref, w2_ref, b2_ref, out_ref,
    img, G, M, meas, samp, wy, wz, gd, sibbuf, S, rbuf, sbuf, xsb, xrb, res, esc, esend, erecv, U,
    W1A, W1B, W2, b1_s, w2_s, col_s, VA, VB, hacc, hid, osc,
    xs, xr, rs, rr, cs, cr, s1s, s1r, s2s, s2r, ls,
    bcs, bcr, brs, brr, bxs, bxr, es, er, us, ur,
):
    s, p, xh, z, c = place()
    sib = slab_of(xh, z, 1 - c)
    xp = slab_of(1 - xh, z, c)
    ring = [slab_of(xh, (z + 1) % 8, c), slab_of(xh, (z + 7) % 8, c)]
    has_up, has_down = s > 0, s < SLABS - 1

    def phase_there(q):
        return jnp.logical_and(p + q >= 0, p + q < PHASES)

    loads = [
        pltpu.make_async_copy(a, b, ls.at[i])
        for i, (a, b) in enumerate(
            (
                (img_h, img),
                (wy_h.at[0], wy.at[0:NY, 0:NY]),
                (wy_h.at[0], wy.at[NY:, NY:]),
                (wy_h.at[1], wy.at[0:NY, NY:]),
                (wz_h.at[0], wz.at[0:NZ, 0:NZ]),
                (wz_h.at[0], wz.at[NZ:, NZ:]),
                (wz_h.at[1], wz.at[NZ:, 0:NZ]),
                (samp_h, samp),
                (meas_h, meas),
            )
        )
    ]
    for load in loads:
        load.start()

    def weights1():
        k = lax.broadcasted_iota(jnp.int32, (270, 1), 0)
        source = ((k // 9 % 3 * 3 + k % 3) * 10 + k // 27) * 16 + k // 3 % 3
        for W, n, wide, first in ((W1A, KA, 8, 0), (W1B, KB, 2, 8)):
            padded = -(-n // 128) * 128
            m = lax.broadcasted_iota(jnp.int32, (1, padded), 1)
            target = (m // (16 * wide) * 10 + first + m // 16 % wide) * 16 + m % 16
            pick = jnp.where(source == target, 1.0, 0.0).astype(BF)
            base = mm(w1_ref[...], pick, NN)
            for zo in range(10):
                turned = base if zo == 0 else pltpu.roll(base, zo, 1)
                W[zo * FEAT : (zo + 1) * FEAT, :] = turned[:, :n].astype(BF)
        same = lax.broadcasted_iota(jnp.int32, (FEAT, FEAT), 0) == lax.broadcasted_iota(
            jnp.int32, (FEAT, FEAT), 1
        )
        bias = jnp.sum(jnp.where(same, b1_ref[...], 0.0), axis=1, keepdims=True)
        for zo in range(10):
            b1_s[zo * FEAT : (zo + 1) * FEAT, :] = bias
        col_s[...] = jnp.zeros_like(col_s)

    def weights2(d):
        k = lax.broadcasted_iota(jnp.int32, (27 * FEAT, 1), 0)
        source = jnp.where(k % 3 == d, k // 3 % 9 * FEAT + k // 27, -1)
        m = lax.broadcasted_iota(jnp.int32, (1, 640), 1)
        pick = jnp.where(source == m, 1.0, 0.0).astype(BF)
        base = mm(w2_ref[...], pick, NN)
        w2_s[...] = jnp.zeros_like(w2_s)
        for a in range(3):
            w2_s[0:10, a * 640 : a * 640 + 192] = base[:, a * 192 : a * 192 + 192]
        base = w2_s[...]
        for zz in range(8):
            turned = base if zz == 0 else pltpu.roll(base, zz * FEAT, 1)
            W2[d * 128 + zz * 16 : d * 128 + zz * 16 + 16, :] = turned.astype(BF)

    barrier = pltpu.get_barrier_semaphore()

    def greet(a, b):
        pl.semaphore_signal(
            barrier, inc=1, device_id={"slab": a, "coil": b}, device_id_type=MESH
        )

    for a in (sib, xp, ring[0], ring[1]):
        greet(a, p)
    for q in range(1, 8):
        greet(s, (p + q) % 8)
    for q in (-2, -1, 0, 1, 2):
        pl.when(jnp.logical_and(has_up, phase_there(q)))(lambda: greet(s - 1, p + q))
        pl.when(jnp.logical_and(has_down, phase_there(q)))(lambda: greet(s + 1, p + q))
    for j in range(4):
        delta = p + 8 * j

        @pl.when(delta != 0)
        def _():
            greet((s + 32 - delta) % 32, p)

    one = lambda cond: jnp.where(cond, 1, 0)
    aside = sum(one(phase_there(q)) for q in OFFSETS)
    pl.semaphore_wait(
        barrier, 15 - one(p == 0) + one(has_up) * (aside + 1) + one(has_down) * (aside + 1)
    )

    plan = Plan()

    def near(j):
        return (s + 32 - (p + 8 * j)) % 32

    def maps_first():
        for j in range(4):
            delta = p + 8 * j
            far = (s + delta) % 32

            @pl.when(delta != 0)
            def _():
                rcopy(maps.at[far], M.at[s], s1s.at[j], s1r.at[j], far, p).start()

            @pl.when(delta == 0)
            def _():
                pltpu.make_async_copy(maps.at[s], M.at[s], ls.at[9]).start()

    def maps_share(j):
        delta = p + 8 * j
        k = near(j)

        @pl.when(delta != 0)
        def _():
            rcopy(maps.at[s], M.at[k], s1s.at[j], s1r.at[j], k, p).wait_recv()

        @pl.when(delta == 0)
        def _():
            pltpu.make_async_copy(maps.at[s], M.at[s], ls.at[9]).wait()

        for q in SHARE:
            maps_copy(j, q, k, 0).start()

    def maps_copy(j, q, k, x):
        half = M.at[k, :, x]
        return rcopy(half, half, s2s.at[x], s2r.at[x, j, q - 1], s, (p + q) % 8)

    def maps_rest():
        for j in range(4):
            for q in SHARE:
                maps_copy(j, q, near(j), 1).start()

    def maps_wait(x):
        for q in SHARE:
            for j in range(4):
                k = (s + 32 - ((p + 8 - q) % 8 + 8 * j)) % 32
                maps_copy(j, q, k, x).wait_recv()

    plan.add("m1", maps_first, after=[("own", 0)],
             sends=[("m1a", "z0", 4), ("m1b", "z1", 4), ("m1", "m1", 4)], rank=-3)
    for j in range(4):
        plan.add(("m2", j), lambda j=j: maps_share(j), after=["m1"], needs=["m1", "m1a", "m1b"],
                 sends=[(("m2", j), "m2", 3.5)], rank=-1)
    plan.add("m2b", maps_rest, after=[("m2", j) for j in range(4)], sends=[("m2b", "m2", 14)], rank=-1)

    def slot(col, dz):
        return slab_of((xh + col) % 2, (z + dz) % 8, c)

    def ring_copy(src, e, col, d, t, k):
        if t == 4:
            src, dst = src.at[d], G.at[e, k, d]
        else:
            dst = G.at[e, k]
        return rcopy(src, dst, rs.at[e], rr.at[e, col, d, t - 1], ring[d], p)

    def core_copy(src, e, k):
        return rcopy(src, G.at[e, k], cs.at[e], cr.at[e], sib, p)

    def own_start(e):
        for d in range(2):
            ring_copy(img_h.at[e], e, 0, d, 1, s).start()

    def own_aside():
        for e in range(E):
            rcopy(img_h.at[e], G.at[e, s], xs.at[e], xr.at[e], xp, p).start()
        for e in range(E):
            core_copy(img_h.at[e], e, s).start()
            G[e, s] = img[e]

    def cross(e):
        rcopy(img_h.at[e], G.at[e, xp], xs.at[e], xr.at[e], xp, p).wait_recv()
        for d in range(2):
            ring_copy(G.at[e, xp], e, 1, d, 1, xp).start()
        core_copy(G.at[e, xp], e, xp).start()

    def hop(e, col, d, t):
        k = slot(col, (8 - t) if d == 0 else t)
        here = G.at[e, k]
        ring_copy(here, e, col, d, t, k).wait_recv()
        if t < 4:
            ring_copy(here, e, col, d, t + 1, k).start()
            core_copy(here, e, k).start()

    def far_slab(e, col):
        for d in range(2):
            hop(e, col, d, 4)
        k = slot(col, 4)
        core_copy(G.at[e, k], e, k).start()

    def gathered(e):
        rcopy(G.at[e, 0:16], G.at[e, 0:16], cs.at[e], cr.at[e], sib, p).wait_recv()

    plan.add("img", lambda: loads[0].wait(), cost=0.3, rank=-2)
    plan.add("aside", own_aside, after=["m1", "img"], sends=[(("x", e), "x", 1) for e in range(E)], rank=-2)
    for e in range(E):
        plan.add(("own", e), lambda e=e: own_start(e), after=["img"] + STAGE.get(e, []),
                 sends=[(("g", e, 0, 0, 1), "z0", 1), (("g", e, 0, 1, 1), "z1", 1)],
                 rank=-2 if e < 1 else e)
        plan.add(("cross", e), lambda e=e: cross(e), after=[("own", e)], needs=[("x", e)],
                 sends=[(("g", e, 1, 0, 1), "z0", 1), (("g", e, 1, 1, 1), "z1", 1)], rank=e)
        for col in range(2):
            for t in range(1, 4):
                for d in range(2):
                    m = ("g", e, col, d, t)
                    plan.add(m, lambda e=e, col=col, d=d, t=t: hop(e, col, d, t), needs=[m],
                             sends=[(("g", e, col, d, t + 1), "z%d" % d, 0.5 if t == 3 else 1)], rank=e)
            plan.add(("far", e, col), lambda e=e, col=col: far_slab(e, col),
                     after=[("g", e, k, d, t) for k in range(col + 1) for d in range(2) for t in range(1, 4)],
                     needs=[("g", e, col, 0, 4), ("g", e, col, 1, 4)],
                     sends=[(("far", e, col), "c", 1)], rank=e)
        plan.add(("full", e), lambda e=e: gathered(e), after=[("far", e, 0), ("far", e, 1)],
                 needs=[("far", e, 0), ("far", e, 1)], rank=e)

    def tables_wait():
        for load in loads[1:]:
            load.wait()
        wy[NY:, 0:NY] = -wy[0:NY, NY:]
        wz[0:NZ, NZ:] = -wz[NZ:, 0:NZ]
        maps_wait(0)

    plan.add("tables", tables_wait, after=[("m2", j) for j in range(4)],
             needs=[("m2", j) for j in range(4)], rank=0)

    plan.add("maps1", lambda: maps_wait(1), needs=["m2b"], after=["tables"], rank=0)
    plan.add("w1", weights1, after=[("own", 1)], cost=2.0, rank=6)
    for d in range(3):
        plan.add(("w2", d), lambda d=d: weights2(d), after=["w1"], cost=1.8, rank=7)

    def block(e, x):
        mask = samp[e].astype(F32)
        wide = lambda v: v.astype(F32).reshape(NZ, NY)
        mr, mi = wide(M[:, 0, x]), wide(M[:, 1, x])
        ir, ii = wide(G[e, :, 0, x]), wide(G[e, :, 1, x])
        pr = (mr * ir - mi * ii).astype(BF)
        pi = (mr * ii + mi * ir).astype(BF)
        r = mm(wy[...], jnp.concatenate([pr, pi], axis=1), NT).astype(BF)
        rc = jnp.concatenate([r[:NY], r[NY:]], axis=1)
        sp = mm(rc, wz[...], NN)
        dr = (mask * (sp[:, :NZ] - meas[e, 0, x].astype(F32))).astype(BF)
        di = (mask * (sp[:, NZ:] - meas[e, 1, x].astype(F32))).astype(BF)
        res[:, :NZ] = dr
        res[:, NZ:] = di

    def block_back(e, x):
        wide = lambda v: v.astype(F32).reshape(NZ, NY)
        mr, mi = wide(M[:, 0, x]), wide(M[:, 1, x])
        b = mm(wz[...], res[...], NT).astype(BF)
        bc = jnp.concatenate([b[:NZ], b[NZ:]], axis=1)
        im = mm(bc, wy[...], NN)
        br, bi = im[:, :NY], im[:, NY:]
        cells = (2, 8, 2, 8, NY)
        gd[e, :, :, :, 0, x] = (mr * br + mi * bi).reshape(cells).astype(BF)
        gd[e, :, :, :, 1, x] = (mr * bi - mi * br).reshape(cells).astype(BF)

    def sib_copy(e):
        return rcopy(gd.at[e, :, :, 1 - c], sibbuf.at[e], bcs.at[e], bcr.at[e], sib, p)

    def last_block(e):
        block_back(e, 1)
        sib_copy(e).start()

    def back_copy(h, e, col, d):
        src, dst = sbuf.at[h, col, d, e], rbuf.at[h, col, d, e]
        if h == 0:
            src, dst = src.at[d], dst.at[d]
        return rcopy(src, dst, brs.at[e], brr.at[h, col, d, e], ring[d], p)

    def x_copy(e):
        return rcopy(xsb.at[e], xrb.at[e], bxs.at[e], bxr.at[e], xp, p)

    def pair_sum(e):
        sib_copy(e).wait_recv()
        S[e] = gd[e, :, :, c].astype(F32) + sibbuf[e].astype(F32)
        for col in (1, 0):
            for d in range(2):
                sbuf[0, col, d, e, d] = S[e, (xh + col) % 2, (z + 4) % 8, d].astype(BF)
                back_copy(0, e, col, d).start()

    def back_hop(e, h, col):
        for d in range(2):
            back_copy(h - 1, e, col, d).wait_recv()
            k = 4 - h
            tz = (z + k) % 8 if d == 0 else (z + 8 - k) % 8
            lane = (xh + col) % 2
            if h == 1:
                v = S[e, lane, tz, d] + rbuf[0, col, d, e, d].astype(F32)
                sbuf[1, col, d, e, d] = v.astype(BF)
                sbuf[1, col, d, e, 1 - d] = S[e, lane, tz, 1 - d].astype(BF)
            else:
                v = S[e, lane, tz] + rbuf[h - 1, col, d, e].astype(F32)
                sbuf[h, col, d, e] = v.astype(BF)
            back_copy(h, e, col, d).start()

    def back_end(e, col):
        for d in range(2):
            back_copy(3, e, col, d).wait_recv()
        lane = (xh + col) % 2
        v = S[e, lane, z] + rbuf[3, col, 0, e].astype(F32) + rbuf[3, col, 1, e].astype(F32)
        if col == 1:
            xsb[e] = v.astype(BF)
            x_copy(e).start()
        else:
            S[e, lane, z] = v

    def u_copy(i, e):
        q = OFFSETS[i]
        return rcopy(U.at[2, e], U.at[2 - q, e], us.at[i, e], ur.at[i, e], s, p + q)

    def e_copy(i, q, e):
        k = 5 * i + q + 2
        return rcopy(esend.at[i, e], erecv.at[i, 2 - q, e], es.at[k, e], er.at[k, e], (s + 1, s - 1)[i], p + q)

    def all_halo(act, inward):
        for i, q in enumerate(OFFSETS):
            pl.when(phase_there(-q if inward else q))(lambda: act(lambda e: u_copy(i, e)))
        for i, cond in enumerate((has_up, has_down) if inward else (has_down, has_up)):
            for q in (0, -1, 1, -2, 2):
                both = jnp.logical_and(cond, phase_there(-q if inward else q))
                pl.when(both)(lambda: act(lambda e: e_copy(i, q, e)))

    def update(e):
        x_copy(e).wait_recv()
        g = S[e, xh, z] + xrb[e].astype(F32)
        u = (img[e].astype(F32) - g).astype(BF)
        U[2, e] = u
        v = u.astype(F32)
        for i, first in enumerate((6, 0)):
            for r in range(2):
                for x in range(2):
                    k = 4 * r + 2 * x
                    esc[i, e, k : k + 2] = v[r, x, first : first + 2]
            esend[i, e] = esc[i, e].astype(BF)
        all_halo(lambda copy: copy(e).start(), False)

    lane = lax.broadcasted_iota(jnp.int32, (32, NY), 1)

    def columns(e):
        all_halo(lambda copy: copy(e).wait_recv(), True)
        V, rows, part0 = (VB, 32, 0) if isinstance(e, int) else (VA, 128, e * 32)

        @pl.loop(0, 5)
        def _(q):
            there = jnp.logical_and(p + q >= 2, p + q < PHASES + 2)
            up = jnp.where(has_up, erecv[0, q, e].astype(F32), 0.0)
            down = jnp.where(has_down, erecv[1, q, e].astype(F32), 0.0)
            for x in range(2):
                col_s[:, 2:10] = U[q, e, :, x].astype(F32)
                for r in range(2):
                    k = 4 * r + 2 * x
                    col_s[r, 0:2] = up[k : k + 2]
                    col_s[r, 10:12] = down[k : k + 2]
                v = jnp.where(there, col_s[...].reshape(32, NY), 0.0)
                back = jnp.where(lane == 0, 0.0, pltpu.roll(v, 1, 1))
                ahead = jnp.where(lane == NY - 1, 0.0, pltpu.roll(v, NY - 1, 1))
                for d, part in enumerate((back, v, ahead)):
                    first = pl.multiple_of((q * 3 + d) * rows + part0, 32)
                    V[pl.ds(first, 32), x * NY : (x + 1) * NY] = part.astype(BF)

    def conv_part(t):
        hacc[t] = mm(W1A[...], VA[t * 384 : t * 384 + KA, :], NN) + b1_s[...]

    before = []
    later = ["maps1"]
    for e in range(E):
        for x in range(2):
            plan.add(("dft", e, x), lambda e=e, x=x: block(e, x), after=["tables", ("full", e)] + before + later * x,
                     cost=0.93, rank=20 + e)
            before = [("back", e, x)]
            plan.add(before[0], lambda e=e, x=x: last_block(e) if x else block_back(e, 0),
                     after=[("dft", e, x)], cost=0.93, sends=[(("bc", e), "c", 16)] * x, rank=20 + e)
        plan.add(("pair", e), lambda e=e: pair_sum(e), after=[("back", e, 1)], needs=[("bc", e)], cost=0.25,
                 sends=[(("b", e, col, 0), "z%d" % d, 0.5) for col in (1, 0) for d in range(2)], rank=10 + e)
        for h in range(1, 4):
            for col in (1, 0):
                plan.add(("back", e, h, col), lambda e=e, h=h, col=col: back_hop(e, h, col),
                         needs=[("b", e, col, h - 1)], after=[("pair", e)] + [("back", e, h, 1)] * (1 - col),
                         sends=[(("b", e, col, h), "z%d" % d, 1) for d in range(2)], cost=0.03, rank=10 + e)
        for col in (1, 0):
            plan.add(("end", e, col), lambda e=e, col=col: back_end(e, col), needs=[("b", e, col, 3)],
                     after=[("back", e, 3, col)], sends=[(("bx", e), "x", 1)] * col, cost=0.1, rank=10 + e)
        plan.add(("upd", e), lambda e=e: update(e), needs=[("bx", e)], after=[("end", e, 0)], cost=0.05,
                 sends=[(("e", e), "e", 1), (("u", e), "y", 1)], rank=10 + e)
    plan.add("cols", lambda: pl.loop(0, 4)(columns), needs=[(k, 3) for k in "ue"], after=[("upd", 4)], cost=1.0)
    for t in range(3):
        plan.add(("conv", t), lambda t=t: conv_part(t), after=["cols"], cost=1.9, rank=30)
    plan.add("cols4", lambda: columns(4), needs=[(k, 4) for k in "ue"], after=["cols"], cost=0.25, rank=40)

    plan.run()

    rows = lax.broadcasted_iota(jnp.int32, (640, 2 * NY), 0)
    lowest = jnp.where(s == 0, FEAT, 0)
    highest = jnp.where(s == SLABS - 1, 9 * FEAT, 10 * FEAT)
    for t in range(3):
        there = jnp.logical_and(p + t >= 1, p + t < PHASES + 1)
        h = mm(W1B[...], VB[t * 96 : t * 96 + KB, :], NN) + hacc[t]
        keep = jnp.logical_and(jnp.logical_and(rows >= lowest, rows < highest), there)
        hid[t * 640 : (t + 1) * 640, :] = jnp.where(keep, jnp.maximum(h, 0.0), 0.0).astype(BF)
    o = mm(W2[...], hid[...], NN)
    lane2 = lax.broadcasted_iota(jnp.int32, (128, 2 * NY), 1) % NY
    total = (
        o[128:256]
        + jnp.where(lane2 == 0, 0.0, pltpu.roll(o[:128], 1, 1))
        + jnp.where(lane2 == NY - 1, 0.0, pltpu.roll(o[256:], 2 * NY - 1, 1))
    )
    for k in range(6):
        osc[k] = total[:, k * 128 : (k + 1) * 128]
    for i in range(10):
        for x in range(2):
            second = jnp.concatenate(
                [osc[3 * x + k, pl.ds(i, 8, stride=16), :] for k in range(3)], axis=1
            )
            v = U[2, i // 2, i % 2, x].astype(F32) + second + b2_ref[i]
            out_ref[i // 2, i % 2, x] = v.astype(BF)

    for j in range(4):
        delta = p + 8 * j
        far = (s + delta) % 32

        @pl.when(delta != 0)
        def _():
            rcopy(maps.at[far], M.at[s], s1s.at[j], s1r.at[j], far, p).wait_send()

    for x in range(2):
        rcopy(G.at[0, 0:14], G.at[0, 0:14], s2s.at[x], s2r.at[0, 0, 0], s, p).wait_send()

    @pl.loop(0, E)
    def _(e):
        rcopy(G.at[e, 0:14], G.at[e, 0:14], rs.at[e], cr.at[e], sib, p).wait_send()
        rcopy(G.at[e, 0:16], G.at[e, 0:16], cs.at[e], cr.at[e], sib, p).wait_send()
        rcopy(img_h.at[e], G.at[e, s], xs.at[e], xr.at[e], xp, p).wait_send()
        sib_copy(e).wait_send()
        x_copy(e).wait_send()
        rcopy(G.at[e, 0:14], G.at[e, 0:14], brs.at[e], cr.at[e], sib, p).wait_send()
        all_halo(lambda copy: copy(e).wait_send(), False)


def whole_step(img, maps, meas, samp, wy, wz, w1, b1, w2, b2):
    sem = pltpu.SemaphoreType.DMA
    vm = pl.BlockSpec(memory_space=pltpu.VMEM)
    far = pl.BlockSpec(memory_space=pl.ANY)
    v = pltpu.VMEM
    return pl.pallas_call(
        kernel,
        out_shape=jax.ShapeDtypeStruct((E, 2, 2, 8, NY), BF),
        in_specs=[far] * 6 + [vm] * 3 + [pl.BlockSpec(memory_space=pltpu.SMEM)],
        out_specs=vm,
        scratch_shapes=[
            v((E, 2, 2, 8, NY), BF),
            v((E, SLABS, 2, 2, 8, NY), BF),
            v((SLABS, 2, 2, 8, NY), BF),
            v((E, 2, 2, NY, NZ), BF),
            v((E, NY, NZ), jnp.int32),
            v((2 * NY, 2 * NY), BF),
            v((2 * NZ, 2 * NZ), BF),
            v((E, 2, 8, 2, 2, 2, 8, NY), BF),
            v((E, 2, 8, 2, 2, 8, NY), BF),
            v((E, 2, 8, 2, 2, 8, NY), F32),
            v((4, 2, 2, E, 2, 2, 8, NY), BF),
            v((4, 2, 2, E, 2, 2, 8, NY), BF),
            v((E, 2, 2, 8, NY), BF),
            v((E, 2, 2, 8, NY), BF),
            v((NY, 2 * NZ), BF),
            v((2, E, 8, NY), F32),
            v((2, E, 8, NY), BF),
            v((2, 5, E, 8, NY), BF),
            v((5, E, 2, 2, 8, NY), BF),
            v((640, KA), BF),
            v((640, KB), BF),
            v((384, K2), BF),
            v((640, 1), F32),
            v((16, K2), F32),
            v((2, 16, NY), F32),
            v((15 * 128, 2 * NY), BF),
            v((15 * 32, 2 * NY), BF),
            v((3, 640, 2 * NY), F32),
            v((1920, 2 * NY), BF),
            v((6, 128, 128), F32),
            sem((E,)), sem((E,)),
            sem((E,)), sem((E, 2, 2, 4)),
            sem((E,)), sem((E,)),
            sem((4,)), sem((4,)),
            sem((2,)), sem((2, 4, 7)),
            sem((10,)),
            sem((E,)), sem((E,)),
            sem((E,)), sem((4, 2, 2, E)),
            sem((E,)), sem((E,)),
            sem((10, E)), sem((10, E)),
            sem((4, E)), sem((4, E)),
        ],
        compiler_params=pltpu.CompilerParams(
            collective_id=0, has_side_effects=True, vmem_limit_bytes=62 * 1024 * 1024
        ),
        name="whole_step",
    )(img, maps, meas, samp, wy, wz, w1, b1, w2, b2)


def on_device(
    current_image,
    coil_maps,
    measured,
    sampling,
    first_weight,
    first_bias,
    second_weight,
    second_bias,
):
    wy, wz = tables()
    out = whole_step(
        current_image[0], coil_maps, measured[0, 0], sampling[0],
        jnp.asarray(wy), jnp.asarray(wz), first_weight.reshape(FEAT, 270),
        first_bias[None], second_weight.reshape(10, 27 * FEAT), second_bias,
    )
    return out[None]


def solution(mesh):
    in_specs = (
        P("coil", None, None, None, "slab", None),
        P(None, None, None, "slab", None),
        P("coil", "slab", None, None, None, None, None),
        P("coil", None, None, None),
        P(),
        P(),
        P(),
        P(),
    )
    out_specs = P("coil", None, None, None, "slab", None)
    return jax.shard_map(
        on_device, mesh=mesh, in_specs=in_specs, out_specs=out_specs, check_vma=False
    )
```

time: 397 us -> 98.3 us (0.25)
  the two profiles are of different devices: /device:TPU:35 before, /device:TPU:24 now
where the time goes in v2:
time: 98.3 us; the launch traced here: 96.4 us
  Pallas kernels  90.7 us (92%)
  local copies, waits for them, and re-layouts  5.65 us (6%)
    pallas_call x1, Pallas kernels, whole_step(): pl.pallas_call(kernel, out_shape=jax.ShapeDtypeStruct((E, 2, 2, 8, NY), B...  90.7 us
    unnamed x2, local copies, waits for them, and re-layouts  2.82 us

profile of v2, /device:TPU:24, one launch (start us, length us, event | category | flops | bytes accessed | tf_op | source)
XLA Modules:
  0.0 96.4 jit_solution(17753032490500816713)
XLA Ops:
  0.0 1.3 %copy.13 = bf16[10,64,3,3,3]{0,4,3,2,1:T(4,128)(2,1)S(1)} copy(bf16[10,64,3,3,3]{1,4,3,2,0:T(4,128)(2,1)} %param.16) | data formatting | bytes 69120 | tf_op args[6]
  1.3 0.3 reshape.7
  1.6 0.8 copy.15.w2_ref
  2.5 0.9 reshape.6
  3.4 0.7 copy.14.w1_ref
  4.1 90.7 %whole_step.1 = bf16[5,2,2,8,384]{4,3,2,1,0:T(8,128)(2,1)} custom-call(bf16[5,2,2,8,384]{4,3,2,1,0:T(8,128)(2,1)} %bitcast.12, bf16[32,2,2,8,384]{4,3,2,1,0:T(8,128)(2,1)} %maps.1, bf16[5,2,2,384,256]{4,3,2,1,0:T(8,128)(2,1)} %bitcast.9, s32[5,384,256]{2,1,0:T(8,128)} %bitcast.10, bf16[2,384,384]{2,1,0:T(8,128)(2,1)} %constant.4.clone.wy_h, ...), custom_call_target="tpu_custom_call" | custom-call | tf_op jit(solution)/shard_map/whole_step/pallas_call | solution.py:549
  94.8 1.6 %copy.17 = bf16[1,5,2,2,8,384]{5,4,3,2,1,0:T(8,128)(2,1)} copy(bf16[1,5,2,2,8,384]{5,4,3,2,1,0:T(8,128)(2,1)} %bitcast.11) | data formatting | bytes 245760

commit v3 on v2

--- a/solution.py
+++ b/solution.py
@@ -63,12 +63,15 @@
     return lax.dot_general(a, b, dims, preferred_element_type=F32)
 
 
-STAGE = {1: ["m1"], 2: [("g", 0, 0, 1, 2)], 3: [("g", 0, 1, 1, 3)], 4: [("far", 0, 1)]}
+STAGE = {1: ["m1"], 2: [("g", 0, 0, 1, 1)], 3: [("g", 0, 1, 1, 1)], 4: [("g", 0, 1, 1, 2)]}
+
+
+Z_FIRST, X_FIRST = (3, 4), (0, 1, 2)
 
 
 class Plan:
     LINKS = {"z0": (0.5, 2.1), "z1": (0.5, 2.1), "x": (0.5, 3.0), "c": (0.05, 1.6),
-             "y": (1.5, 3.2), "e": (0.5, 6.0), "m1": (0.5, 4.0), "m2": (0.3, 3.0)}
+             "y": (2.2, 3.2), "e": (0.5, 6.0), "m1": (0.5, 4.0), "m2": (0.3, 3.0)}
 
     def __init__(self):
         self.tasks = []
@@ -101,7 +104,7 @@
 
 def kernel(
     img_h, maps, meas_h, samp_h, wy_h, wz_h, w1_ref, b1_ref, w2_ref, b2_ref, out_ref,
-    img, G, M, meas, samp, wy, wz, gd, sibbuf, S, rbuf, sbuf, xsb, xrb, res, esc, esend, erecv, U,
+    img, G, M, meas, samp, wy, wz, gd, sibbuf, S, rbuf, sbuf, xsb, xrb, xsb8, xrb8, res, esc, esend, erecv, U,
     W1A, W1B, W2, b1_s, w2_s, col_s, VA, VB, hacc, hid, osc,
     xs, xr, rs, rr, cs, cr, s1s, s1r, s2s, s2r, ls,
     bcs, bcr, brs, brr, bxs, bxr, es, er, us, ur,
@@ -166,7 +169,7 @@
         base = w2_s[...]
         for zz in range(8):
             turned = base if zz == 0 else pltpu.roll(base, zz * FEAT, 1)
-            W2[d * 128 + zz * 16 : d * 128 + zz * 16 + 16, :] = turned.astype(BF)
+            W2[pl.ds(pl.multiple_of(d * 128 + zz * 16, 16), 16), :] = turned.astype(BF)
 
     barrier = pltpu.get_barrier_semaphore()
 
@@ -247,8 +250,8 @@
              sends=[("m1a", "z0", 4), ("m1b", "z1", 4), ("m1", "m1", 4)], rank=-3)
     for j in range(4):
         plan.add(("m2", j), lambda j=j: maps_share(j), after=["m1"], needs=["m1", "m1a", "m1b"],
-                 sends=[(("m2", j), "m2", 3.5)], rank=-1)
-    plan.add("m2b", maps_rest, after=[("m2", j) for j in range(4)], sends=[("m2b", "m2", 14)], rank=-1)
+                 sends=[(("m2", j), "m2", 3.5), (("m2x", j), "x", 2)], rank=-1)
+    plan.add("m2b", maps_rest, after=[("m2", j) for j in range(4)], sends=[("m2b", "m2", 14), ("m2bx", "x", 8)], rank=-1)
 
     def slot(col, dz):
         return slab_of((xh + col) % 2, (z + dz) % 8, c)
@@ -280,19 +283,30 @@
             ring_copy(G.at[e, xp], e, 1, d, 1, xp).start()
         core_copy(G.at[e, xp], e, xp).start()
 
+    def spread(e, k):
+        core_copy(G.at[e, k], e, k).start()
+        if e in Z_FIRST:
+            rcopy(G.at[e, k], G.at[e, k], xs.at[e], xr.at[e], xp, p).start()
+
     def hop(e, col, d, t):
         k = slot(col, (8 - t) if d == 0 else t)
-        here = G.at[e, k]
-        ring_copy(here, e, col, d, t, k).wait_recv()
+        ring_copy(G.at[e, k], e, col, d, t, k).wait_recv()
         if t < 4:
-            ring_copy(here, e, col, d, t + 1, k).start()
-            core_copy(here, e, k).start()
+            ring_copy(G.at[e, k], e, col, d, t + 1, k).start()
+            spread(e, k)
 
     def far_slab(e, col):
         for d in range(2):
             hop(e, col, d, 4)
-        k = slot(col, 4)
-        core_copy(G.at[e, k], e, k).start()
+        spread(e, slot(col, 4))
+
+    def cross_all(e):
+        rcopy(G.at[e, 0:8], G.at[e, 0:8], xs.at[e], xr.at[e], xp, p).wait_recv()
+
+        @pl.loop(0, 8)
+        def _(zz):
+            k = slab_of(1 - xh, zz, c)
+            core_copy(G.at[e, k], e, k).start()
 
     def gathered(e):
         rcopy(G.at[e, 0:16], G.at[e, 0:16], cs.at[e], cr.at[e], sib, p).wait_recv()
@@ -303,19 +317,26 @@
         plan.add(("own", e), lambda e=e: own_start(e), after=["img"] + STAGE.get(e, []),
                  sends=[(("g", e, 0, 0, 1), "z0", 1), (("g", e, 0, 1, 1), "z1", 1)],
                  rank=-2 if e < 1 else e)
-        plan.add(("cross", e), lambda e=e: cross(e), after=[("own", e)], needs=[("x", e)],
-                 sends=[(("g", e, 1, 0, 1), "z0", 1), (("g", e, 1, 1, 1), "z1", 1)], rank=e)
-        for col in range(2):
+        direct = e in Z_FIRST
+        if direct:
+            xneeds = [("xg", e, t, d) for t in range(1, 4) for d in range(2)] + [("xg", e, 4)]
+            plan.add(("cross", e), lambda e=e: cross_all(e), needs=xneeds, after=[("far", e, 0)],
+                     sends=[(("far", e, 1), "c", 8)], rank=e)
+        else:
+            plan.add(("cross", e), lambda e=e: cross(e), after=[("own", e)], needs=[("x", e)],
+                     sends=[(("g", e, 1, 0, 1), "z0", 1), (("g", e, 1, 1, 1), "z1", 1)], rank=e)
+        for col in range(1 if direct else 2):
             for t in range(1, 4):
                 for d in range(2):
                     m = ("g", e, col, d, t)
                     plan.add(m, lambda e=e, col=col, d=d, t=t: hop(e, col, d, t), needs=[m],
-                             sends=[(("g", e, col, d, t + 1), "z%d" % d, 0.5 if t == 3 else 1)], rank=e)
+                             sends=[(("g", e, col, d, t + 1), "z%d" % d, 0.5 if t == 3 else 1)]
+                             + [(("xg", e, t, d), "x", 1)] * direct, rank=e)
             plan.add(("far", e, col), lambda e=e, col=col: far_slab(e, col),
                      after=[("g", e, k, d, t) for k in range(col + 1) for d in range(2) for t in range(1, 4)],
                      needs=[("g", e, col, 0, 4), ("g", e, col, 1, 4)],
-                     sends=[(("far", e, col), "c", 1)], rank=e)
-        plan.add(("full", e), lambda e=e: gathered(e), after=[("far", e, 0), ("far", e, 1)],
+                     sends=[(("far", e, col), "c", 1)] + [(("xg", e, 4), "x", 1)] * direct, rank=e)
+        plan.add(("full", e), lambda e=e: gathered(e), after=[("far", e, 0), ("cross" if direct else "far", e, 1)[: 3 - direct]],
                  needs=[("far", e, 0), ("far", e, 1)], rank=e)
 
     def tables_wait():
@@ -330,8 +351,7 @@
 
     plan.add("maps1", lambda: maps_wait(1), needs=["m2b"], after=["tables"], rank=0)
     plan.add("w1", weights1, after=[("own", 1)], cost=2.0, rank=6)
-    for d in range(3):
-        plan.add(("w2", d), lambda d=d: weights2(d), after=["w1"], cost=1.8, rank=7)
+    plan.add("w2", lambda: pl.loop(0, 3)(weights2), after=["w1"], cost=1.6, rank=7)
 
     def block(e, x):
         mask = samp[e].astype(F32)
@@ -378,10 +398,25 @@
     def pair_sum(e):
         sib_copy(e).wait_recv()
         S[e] = gd[e, :, :, c].astype(F32) + sibbuf[e].astype(F32)
-        for col in (1, 0):
+        if e in X_FIRST:
+            xsb8[e] = S[e, 1 - xh].astype(BF)
+            x_copy8(e).start()
+        else:
+            first_hop(e, (1, 0))
+
+    def first_hop(e, cols):
+        for col in cols:
             for d in range(2):
                 sbuf[0, col, d, e, d] = S[e, (xh + col) % 2, (z + 4) % 8, d].astype(BF)
                 back_copy(0, e, col, d).start()
+
+    def x_copy8(e):
+        return rcopy(xsb8.at[e], xrb8.at[e], bxs.at[e], bxr.at[e], xp, p)
+
+    def x_sum(e):
+        x_copy8(e).wait_recv()
+        S[e, xh] = S[e, xh] + xrb8[e].astype(F32)
+        first_hop(e, (0,))
 
     def back_hop(e, h, col):
         for d in range(2):
@@ -426,8 +461,10 @@
                 pl.when(both)(lambda: act(lambda e: e_copy(i, q, e)))
 
     def update(e):
-        x_copy(e).wait_recv()
-        g = S[e, xh, z] + xrb[e].astype(F32)
+        g = S[e, xh, z]
+        if e not in X_FIRST:
+            x_copy(e).wait_recv()
+            g = g + xrb[e].astype(F32)
         u = (img[e].astype(F32) - g).astype(BF)
         U[2, e] = u
         v = u.astype(F32)
@@ -464,7 +501,8 @@
                     V[pl.ds(first, 32), x * NY : (x + 1) * NY] = part.astype(BF)
 
     def conv_part(t):
-        hacc[t] = mm(W1A[...], VA[t * 384 : t * 384 + KA, :], NN) + b1_s[...]
+        cells = VA[pl.ds(pl.multiple_of(t * 384, 384), KA), :]
+        hacc[t] = mm(W1A[...], cells, NN) + b1_s[...]
 
     before = []
     later = ["maps1"]
@@ -475,21 +513,28 @@
             before = [("back", e, x)]
             plan.add(before[0], lambda e=e, x=x: last_block(e) if x else block_back(e, 0),
                      after=[("dft", e, x)], cost=0.93, sends=[(("bc", e), "c", 16)] * x, rank=20 + e)
-        plan.add(("pair", e), lambda e=e: pair_sum(e), after=[("back", e, 1)], needs=[("bc", e)], cost=0.25,
-                 sends=[(("b", e, col, 0), "z%d" % d, 0.5) for col in (1, 0) for d in range(2)], rank=10 + e)
+        cols = (0,) if e in X_FIRST else (1, 0)
+        starts = [(("b", e, col, 0), "z%d" % d, 0.5) for col in cols for d in range(2)]
+        if e in X_FIRST:
+            plan.add(("pair", e), lambda e=e: pair_sum(e), after=[("back", e, 1)], needs=[("bc", e)], cost=0.25,
+                     sends=[(("bx", e), "x", 8)], rank=10 + e)
+            plan.add(("xsum", e), lambda e=e: x_sum(e), after=[("pair", e)], needs=[("bx", e)], cost=0.15,
+                     sends=starts, rank=10 + e)
+        else:
+            plan.add(("pair", e), lambda e=e: pair_sum(e), after=[("back", e, 1)], needs=[("bc", e)], cost=0.25,
+                     sends=starts, rank=10 + e)
         for h in range(1, 4):
-            for col in (1, 0):
+            for col in cols:
                 plan.add(("back", e, h, col), lambda e=e, h=h, col=col: back_hop(e, h, col),
-                         needs=[("b", e, col, h - 1)], after=[("pair", e)] + [("back", e, h, 1)] * (1 - col),
+                         needs=[("b", e, col, h - 1)], after=[("pair", e)] + [("back", e, h, 1)] * ((1 - col) * (len(cols) - 1)),
                          sends=[(("b", e, col, h), "z%d" % d, 1) for d in range(2)], cost=0.03, rank=10 + e)
-        for col in (1, 0):
+        for col in cols:
             plan.add(("end", e, col), lambda e=e, col=col: back_end(e, col), needs=[("b", e, col, 3)],
                      after=[("back", e, 3, col)], sends=[(("bx", e), "x", 1)] * col, cost=0.1, rank=10 + e)
         plan.add(("upd", e), lambda e=e: update(e), needs=[("bx", e)], after=[("end", e, 0)], cost=0.05,
                  sends=[(("e", e), "e", 1), (("u", e), "y", 1)], rank=10 + e)
     plan.add("cols", lambda: pl.loop(0, 4)(columns), needs=[(k, 3) for k in "ue"], after=[("upd", 4)], cost=1.0)
-    for t in range(3):
-        plan.add(("conv", t), lambda t=t: conv_part(t), after=["cols"], cost=1.9, rank=30)
+    plan.add("conv", lambda: pl.loop(0, 3)(conv_part), after=["cols"], cost=5.6, rank=30)
     plan.add("cols4", lambda: columns(4), needs=[(k, 4) for k in "ue"], after=["cols"], cost=0.25, rank=40)
 
     plan.run()
@@ -497,11 +542,16 @@
     rows = lax.broadcasted_iota(jnp.int32, (640, 2 * NY), 0)
     lowest = jnp.where(s == 0, FEAT, 0)
     highest = jnp.where(s == SLABS - 1, 9 * FEAT, 10 * FEAT)
-    for t in range(3):
+
+    @pl.loop(0, 3)
+    def _(t):
         there = jnp.logical_and(p + t >= 1, p + t < PHASES + 1)
-        h = mm(W1B[...], VB[t * 96 : t * 96 + KB, :], NN) + hacc[t]
+        cells = VB[pl.ds(pl.multiple_of(t * 96, 96), KB), :]
+        h = mm(W1B[...], cells, NN) + hacc[t]
         keep = jnp.logical_and(jnp.logical_and(rows >= lowest, rows < highest), there)
-        hid[t * 640 : (t + 1) * 640, :] = jnp.where(keep, jnp.maximum(h, 0.0), 0.0).astype(BF)
+        first = pl.multiple_of(t * 640, 640)
+        hid[pl.ds(first, 640), :] = jnp.where(keep, jnp.maximum(h, 0.0), 0.0).astype(BF)
+
     o = mm(W2[...], hid[...], NN)
     lane2 = lax.broadcasted_iota(jnp.int32, (128, 2 * NY), 1) % NY
     total = (
@@ -530,14 +580,19 @@
     for x in range(2):
         rcopy(G.at[0, 0:14], G.at[0, 0:14], s2s.at[x], s2r.at[0, 0, 0], s, p).wait_send()
 
+    def left(e, n, sem):
+        rcopy(G.at[e, 0:n], G.at[e, 0:n], sem.at[e], cr.at[e], sib, p).wait_send()
+
+    for e in range(E):
+        left(e, 7 if e in Z_FIRST else 14, rs)
+        left(e, 8 if e in Z_FIRST else 1, xs)
+        left(e, 7 if e in X_FIRST else 14, brs)
+        left(e, 8 if e in X_FIRST else 1, bxs)
+
     @pl.loop(0, E)
     def _(e):
-        rcopy(G.at[e, 0:14], G.at[e, 0:14], rs.at[e], cr.at[e], sib, p).wait_send()
-        rcopy(G.at[e, 0:16], G.at[e, 0:16], cs.at[e], cr.at[e], sib, p).wait_send()
-        rcopy(img_h.at[e], G.at[e, s], xs.at[e], xr.at[e], xp, p).wait_send()
+        left(e, 16, cs)
         sib_copy(e).wait_send()
-        x_copy(e).wait_send()
-        rcopy(G.at[e, 0:14], G.at[e, 0:14], brs.at[e], cr.at[e], sib, p).wait_send()
         all_halo(lambda copy: copy(e).wait_send(), False)
 
 
@@ -566,6 +621,8 @@
             v((4, 2, 2, E, 2, 2, 8, NY), BF),
             v((E, 2, 2, 8, NY), BF),
             v((E, 2, 2, 8, NY), BF),
+            v((3, 8, 2, 2, 8, NY), BF),
+            v((3, 8, 2, 2, 8, NY), BF),
             v((NY, 2 * NZ), BF),
             v((2, E, 8, NY), F32),
             v((2, E, 8, NY), BF),

time: 98.3 us -> 96.8 us (0.985); the launches traced: 96.4 us -> 96.6 us
  no operation moved by 1% of the time
where the time goes in v3:
time: 96.8 us; the launch traced here: 96.6 us
  Pallas kernels  90.9 us (94%)
  local copies, waits for them, and re-layouts  5.65 us (6%)
    pallas_call x1, Pallas kernels, whole_step(): pl.pallas_call(kernel, out_shape=jax.ShapeDtypeStruct((E, 2, 2, 8, NY), B...  90.9 us
    unnamed x2, local copies, waits for them, and re-layouts  2.82 us

profile of v3, /device:TPU:24, one launch (start us, length us, event | category | flops | bytes accessed | tf_op | source)
XLA Modules:
  0.0 96.6 jit_solution(16882955216675722858)
XLA Ops:
  0.0 1.3 %copy.13 = bf16[10,64,3,3,3]{0,4,3,2,1:T(4,128)(2,1)S(1)} copy(bf16[10,64,3,3,3]{1,4,3,2,0:T(4,128)(2,1)} %param.16) | data formatting | bytes 69120 | tf_op args[6]
  1.3 0.3 reshape.7
  1.6 0.8 copy.15.w2_ref
  2.5 0.9 reshape.6
  3.4 0.7 copy.14.w1_ref
  4.1 90.9 %whole_step.1 = bf16[5,2,2,8,384]{4,3,2,1,0:T(8,128)(2,1)} custom-call(bf16[5,2,2,8,384]{4,3,2,1,0:T(8,128)(2,1)} %bitcast.12, bf16[32,2,2,8,384]{4,3,2,1,0:T(8,128)(2,1)} %maps.1, bf16[5,2,2,384,256]{4,3,2,1,0:T(8,128)(2,1)} %bitcast.9, s32[5,384,256]{2,1,0:T(8,128)} %bitcast.10, bf16[2,384,384]{2,1,0:T(8,128)(2,1)} %constant.4.clone.wy_h, ...), custom_call_target="tpu_custom_call" | custom-call | tf_op jit(solution)/shard_map/whole_step/pallas_call | solution.py:604
  95.0 1.6 %copy.17 = bf16[1,5,2,2,8,384]{5,4,3,2,1,0:T(8,128)(2,1)} copy(bf16[1,5,2,2,8,384]{5,4,3,2,1,0:T(8,128)(2,1)} %bitcast.11) | data formatting | bytes 245760

commit v4 on v3

--- a/solution.py
+++ b/solution.py
@@ -16,7 +16,8 @@
 SLABS, PHASES = 32, 8
 NT = (((1,), (1,)), ((), ()))
 NN = (((1,), (0,)), ((), ()))
-OFFSETS = (1, -1, 2, -2)
+TN = (((0,), (0,)), ((), ()))
+OFFSETS = (2, -2, 1, -1)
 SHARE = (4, 1, 7, 3, 5, 2, 6)
 KA, KB = 9 * 8 * 16, 9 * 2 * 16
 K2 = 3 * 10 * FEAT
@@ -103,9 +104,9 @@
 
 
 def kernel(
-    img_h, maps, meas_h, samp_h, wy_h, wz_h, w1_ref, b1_ref, w2_ref, b2_ref, out_ref,
+    img_h, maps, meas_h, samp_h, wy_h, wz_h, w1_h, b1_ref, w2_h, b2_ref, out_ref,
     img, G, M, meas, samp, wy, wz, gd, sibbuf, S, rbuf, sbuf, xsb, xrb, xsb8, xrb8, res, esc, esend, erecv, U,
-    W1A, W1B, W2, b1_s, w2_s, col_s, VA, VB, hacc, hid, osc,
+    w1_ref, w2_ref, W1A, W1B, W2, b1_s, w2_s, col_s, VA, VB, hacc, hid, osc,
     xs, xr, rs, rr, cs, cr, s1s, s1r, s2s, s2r, ls,
     bcs, bcr, brs, brr, bxs, bxr, es, er, us, ur,
 ):
@@ -131,6 +132,8 @@
                 (wz_h.at[1], wz.at[NZ:, 0:NZ]),
                 (samp_h, samp),
                 (meas_h, meas),
+                (w1_h, w1_ref),
+                (w2_h, w2_ref),
             )
         )
     ]
@@ -138,6 +141,8 @@
         load.start()
 
     def weights1():
+        for load in loads[9:]:
+            load.wait()
         k = lax.broadcasted_iota(jnp.int32, (270, 1), 0)
         source = ((k // 9 % 3 * 3 + k % 3) * 10 + k // 27) * 16 + k // 3 % 3
         for W, n, wide, first in ((W1A, KA, 8, 0), (W1B, KB, 2, 8)):
@@ -145,7 +150,7 @@
             m = lax.broadcasted_iota(jnp.int32, (1, padded), 1)
             target = (m // (16 * wide) * 10 + first + m // 16 % wide) * 16 + m % 16
             pick = jnp.where(source == target, 1.0, 0.0).astype(BF)
-            base = mm(w1_ref[...], pick, NN)
+            base = mm(w1_ref[...], pick, TN)
             for zo in range(10):
                 turned = base if zo == 0 else pltpu.roll(base, zo, 1)
                 W[zo * FEAT : (zo + 1) * FEAT, :] = turned[:, :n].astype(BF)
@@ -162,7 +167,7 @@
         source = jnp.where(k % 3 == d, k // 3 % 9 * FEAT + k // 27, -1)
         m = lax.broadcasted_iota(jnp.int32, (1, 640), 1)
         pick = jnp.where(source == m, 1.0, 0.0).astype(BF)
-        base = mm(w2_ref[...], pick, NN)
+        base = mm(w2_ref[...], pick, TN)
         w2_s[...] = jnp.zeros_like(w2_s)
         for a in range(3):
             w2_s[0:10, a * 640 : a * 640 + 192] = base[:, a * 192 : a * 192 + 192]
@@ -214,7 +219,7 @@
 
             @pl.when(delta == 0)
             def _():
-                pltpu.make_async_copy(maps.at[s], M.at[s], ls.at[9]).start()
+                pltpu.make_async_copy(maps.at[s], M.at[s], ls.at[11]).start()
 
     def maps_share(j):
         delta = p + 8 * j
@@ -226,7 +231,7 @@
 
         @pl.when(delta == 0)
         def _():
-            pltpu.make_async_copy(maps.at[s], M.at[s], ls.at[9]).wait()
+            pltpu.make_async_copy(maps.at[s], M.at[s], ls.at[11]).wait()
 
         for q in SHARE:
             maps_copy(j, q, k, 0).start()
@@ -340,7 +345,7 @@
                  needs=[("far", e, 0), ("far", e, 1)], rank=e)
 
     def tables_wait():
-        for load in loads[1:]:
+        for load in loads[1:9]:
             load.wait()
         wy[NY:, 0:NY] = -wy[0:NY, NY:]
         wz[0:NZ, NZ:] = -wz[NZ:, 0:NZ]
@@ -453,12 +458,12 @@
         return rcopy(esend.at[i, e], erecv.at[i, 2 - q, e], es.at[k, e], er.at[k, e], (s + 1, s - 1)[i], p + q)
 
     def all_halo(act, inward):
+        for i, cond in enumerate((has_up, has_down) if inward else (has_down, has_up)):
+            for q in (-2, 2, -1, 1, 0):
+                both = jnp.logical_and(cond, phase_there(-q if inward else q))
+                pl.when(both)(lambda: act(lambda e: e_copy(i, q, e)))
         for i, q in enumerate(OFFSETS):
             pl.when(phase_there(-q if inward else q))(lambda: act(lambda e: u_copy(i, e)))
-        for i, cond in enumerate((has_up, has_down) if inward else (has_down, has_up)):
-            for q in (0, -1, 1, -2, 2):
-                both = jnp.logical_and(cond, phase_there(-q if inward else q))
-                pl.when(both)(lambda: act(lambda e: e_copy(i, q, e)))
 
     def update(e):
         g = S[e, xh, z]
@@ -604,7 +609,7 @@
     return pl.pallas_call(
         kernel,
         out_shape=jax.ShapeDtypeStruct((E, 2, 2, 8, NY), BF),
-        in_specs=[far] * 6 + [vm] * 3 + [pl.BlockSpec(memory_space=pltpu.SMEM)],
+        in_specs=[far] * 7 + [vm, far, pl.BlockSpec(memory_space=pltpu.SMEM)],
         out_specs=vm,
         scratch_shapes=[
             v((E, 2, 2, 8, NY), BF),
@@ -628,6 +633,8 @@
             v((2, E, 8, NY), BF),
             v((2, 5, E, 8, NY), BF),
             v((5, E, 2, 2, 8, NY), BF),
+            v((270, FEAT), BF),
+            v((27 * FEAT, 10), BF),
             v((640, KA), BF),
             v((640, KB), BF),
             v((384, K2), BF),
@@ -644,7 +651,7 @@
             sem((E,)), sem((E,)),
             sem((4,)), sem((4,)),
             sem((2,)), sem((2, 4, 7)),
-            sem((10,)),
+            sem((12,)),
             sem((E,)), sem((E,)),
             sem((E,)), sem((4, 2, 2, E)),
             sem((E,)), sem((E,)),
@@ -671,8 +678,8 @@
     wy, wz = tables()
     out = whole_step(
         current_image[0], coil_maps, measured[0, 0], sampling[0],
-        jnp.asarray(wy), jnp.asarray(wz), first_weight.reshape(FEAT, 270),
-        first_bias[None], second_weight.reshape(10, 27 * FEAT), second_bias,
+        jnp.asarray(wy), jnp.asarray(wz), first_weight.transpose(1, 2, 3, 4, 0).reshape(270, FEAT),
+        first_bias[None], second_weight.transpose(1, 2, 3, 4, 0).reshape(27 * FEAT, 10), second_bias,
     )
     return out[None]
 

time: 96.8 us -> 96.9 us (level)
    transpose x0 -> x1, local copies, waits for them, and re-layouts: none -> 1.26 us  [on_device(): second_weight.transpose(1, 2, 3, 4, 0).reshape(27 * FEAT, 10)]
    unnamed x2 -> x1, local copies, waits for them, and re-layouts: 2.82 us -> 1.56 us
    reshape x4 -> x2, local copies, waits for them, and re-layouts: 2.83 us -> 2.68 us  [the longest x1 1.58 us: on_device(): first_weight.transpose(1, 2, 3, 4, 0).reshape(270, FEAT)]
where the time goes in v4:
time: 96.9 us; the launch traced here: 96.7 us
  Pallas kernels  91.2 us (94%)
  local copies, waits for them, and re-layouts  5.5 us (6%)
    pallas_call x1, Pallas kernels, whole_step(): pl.pallas_call(kernel, out_shape=jax.ShapeDtypeStruct((E, 2, 2, 8, NY), B...  91.2 us

profile of v4, /device:TPU:24, one launch (start us, length us, event | category | flops | bytes accessed | tf_op | source)
XLA Modules:
  0.0 96.7 jit_solution(10100436291225246308)
XLA Ops:
  0.0 1.3 %copy.12 = bf16[64,3,3,3,10]{4,3,2,1,0:T(4,128)(2,1)S(1)} copy(bf16[64,3,3,3,10]{0,3,2,1,4:T(4,128)(2,1)} %bitcast.12) | data formatting | bytes 69120 | tf_op jit(solution)/shard_map/transpose | solution.py:682
  1.3 1.1 %reshape.7.w2_h = bf16[1728,10]{1,0:T(8,128)(2,1)} reshape(bf16[64,3,3,3,10]{4,3,2,1,0:T(4,128)(2,1)S(1)} %copy.12) | data formatting | bytes 69120 | tf_op jit(solution)/shard_map/reshape | solution.py:682
  2.4 1.6 %reshape.6.w1_h = bf16[270,64]{1,0:T(8,128)(2,1)} reshape(bf16[10,3,3,3,64]{4,3,2,1,0:T(4,128)(2,1)} %bitcast.11) | data formatting | bytes 69120 | tf_op jit(solution)/shard_map/reshape | solution.py:681
  4.0 91.2 %whole_step.1 = bf16[5,2,2,8,384]{4,3,2,1,0:T(8,128)(2,1)} custom-call(bf16[5,2,2,8,384]{4,3,2,1,0:T(8,128)(2,1)} %bitcast.10, bf16[32,2,2,8,384]{4,3,2,1,0:T(8,128)(2,1)} %maps.1, bf16[5,2,2,384,256]{4,3,2,1,0:T(8,128)(2,1)} %bitcast.7, s32[5,384,256]{2,1,0:T(8,128)} %bitcast.8, bf16[2,384,384]{2,1,0:T(8,128)(2,1)} %constant.4.clone.wy_h, ...), custom_call_target="tpu_custom_call" | custom-call | tf_op jit(solution)/shard_map/whole_step/pallas_call | solution.py:609
  95.1 1.6 %copy.14 = bf16[1,5,2,2,8,384]{5,4,3,2,1,0:T(8,128)(2,1)} copy(bf16[1,5,2,2,8,384]{5,4,3,2,1,0:T(8,128)(2,1)} %bitcast.9) | data formatting | bytes 245760
